TPU v7x, 512 devices: a whole 4x4x16 slice. The times are simulated.
512 devices in a mesh: dp: 64 (over y, z), mp: 8 (over x, core).
Axes of the slice: x: 4, y: 4, z: 16, core: 2. Of those that a mesh axis runs over, the one named last changes fastest.
Arguments:
- preact: float32 [64, 16, 16, 1024], P('dp', None, None, 'mp'), may hold values from -6 to 6
- weights: float32 [512, 9, 1024], P('mp'), may hold values from -0.0625 to 0.0625
- cotangent: float32 [64, 16, 16, 512], P('dp', None, None, 'mp'), may hold values from -24 to 24
Outputs:
- output: float32 [64, 16, 16, 512], P('dp', None, None, 'mp')
- input_grad: float32 [64, 16, 16, 1024], P('dp', None, None, 'mp')
- weight_grad: float32 [512, 9216], P('mp', 'dp')
All inputs are finite; a program needn't handle non-finite values.
Results may differ from a plain program's by a relative error of at most 0.0003.
Values sent between devices are 32-bit elements; how exact they have to be, the bound alone decides.
A program may use at most 64 MiB of HBM per device.

v0:
```python
import jax
import jax.numpy as jnp
from jax import lax
from jax.sharding import Mesh
from jax.sharding import PartitionSpec as P

DP = ("dp_0", "dp_1")
MP = ("mp_0", "mp_1")


highest = lax.Precision.HIGHEST
epsilon = 1e-06


def copy_for_each(x, axis):
    copies = jnp.broadcast_to(x, (lax.axis_size(axis), *x.shape))
    return lax.all_to_all(copies, axis, split_axis=0, concat_axis=0, tiled=True)


def of_everyone(x, axis):
    everything = copy_for_each(x, axis)
    return jnp.sum(everything, axis=0)


def over_axes(x, axes):
    far, near = axes
    return of_everyone(of_everyone(x, near), far)


def laid_out(parts, dim):
    parts = jnp.moveaxis(parts, 0, dim)
    lengths = parts.shape
    return parts.reshape(*lengths[:dim], lengths[dim] * lengths[dim + 1], *lengths[dim + 2 :])


def gather_directly(x, axis, dim):
    parts = copy_for_each(x, axis)
    return laid_out(parts, dim)


def in_blocks(x, dim, devices):
    lengths = x.shape
    parts = x.reshape(*lengths[:dim], devices, lengths[dim] // devices, *lengths[dim + 1 :])
    return jnp.moveaxis(parts, dim, 0)


def summed_on_arrival(x, axis, dim):
    parts = in_blocks(x, dim, lax.axis_size(axis))
    arrived = lax.all_to_all(parts, axis, split_axis=0, concat_axis=0, tiled=True)
    return arrived.sum(axis=0)


def activate(values):
    return 0.5 * values * (1.0 + lax.erf(values * 0.7071067811865476))


def gelu_slope(values):
    return (
        0.5 * (1.0 + lax.erf(values * 0.7071067811865476))
        + values * jnp.exp(-0.5 * values * values) * 0.3989422804014327
    )


def pad_image(values):
    return jnp.pad(values, ((0, 0), (1, 1), (1, 1), (0, 0)))


def convolve_piece(activity, filters):
    extent = activity.shape[1]
    padded = pad_image(activity)
    summed = jnp.zeros(activity.shape[:3] + (filters.shape[0],), jnp.float32)
    for kernel_tap in range(9):
        row_shift, column_shift = divmod(kernel_tap, 3)
        window = padded[:, row_shift : row_shift + extent, column_shift : column_shift + extent, :]
        summed = summed + jnp.einsum(
            "nhwc,oc->nhwo", window, filters[:, kernel_tap, :], precision=highest
        )
    return summed


def weight_piece(activity, upstream):
    extent = activity.shape[1]
    padded = pad_image(activity)
    tap_grads = []
    for kernel_tap in range(9):
        row_shift, column_shift = divmod(kernel_tap, 3)
        window = padded[:, row_shift : row_shift + extent, column_shift : column_shift + extent, :]
        tap_grads.append(jnp.einsum("nhwo,nhwc->oc", upstream, window, precision=highest))
    return jnp.stack(tap_grads, 1)


def input_partial(upstream, filters):
    extent = upstream.shape[1]
    padded = pad_image(upstream)
    summed = jnp.zeros(upstream.shape[:3] + (filters.shape[2],), jnp.float32)
    for kernel_tap in range(9):
        row_shift, column_shift = divmod(kernel_tap, 3)
        window = padded[
            :,
            2 - row_shift : 2 - row_shift + extent,
            2 - column_shift : 2 - column_shift + extent,
            :,
        ]
        summed = summed + jnp.einsum(
            "nhwo,oc->nhwc", window, filters[:, kernel_tap, :], precision=highest
        )
    return summed


def adasum_columns(gradient):
    filter_count = gradient.shape[0]
    groups = lax.axis_size(DP)
    breadth = gradient.shape[1] * gradient.shape[2] // groups
    blocks = gradient.reshape(filter_count, groups, breadth)
    spread = lax.all_to_all(blocks, DP, split_axis=1, concat_axis=1, tiled=True)
    while spread.shape[1] > 1:
        paired = spread.reshape(filter_count, spread.shape[1] // 2, 2, breadth)
        leading = paired[:, :, 0]
        second = paired[:, :, 1]
        moments = jnp.stack(
            [
                jnp.sum(leading * second, (0, 2)),
                jnp.sum(leading * leading, (0, 2)),
                jnp.sum(second * second, (0, 2)),
            ],
            1,
        )
        totals = over_axes(moments, (("dp_0", "dp_1"), ("mp_0", "mp_1")))
        cross = totals[:, 0][None, :, None]
        lead_sq = totals[:, 1][None, :, None]
        second_sq = totals[:, 2][None, :, None]
        spread = (1.0 - cross / (2.0 * (lead_sq + epsilon))) * leading + (
            1.0 - cross / (2.0 * (second_sq + epsilon))
        ) * second
    return spread.reshape(filter_count, breadth)


def local(preact, weights, cotangent):
    activity = activate(preact)
    positions = preact.shape[0] * preact.shape[1] * preact.shape[2]
    everything = gather_directly(activity, MP, 3)
    output = convolve_piece(everything, weights)
    gradient = weight_piece(everything, cotangent)
    partial_sum = input_partial(cotangent, weights)
    input_grad = summed_on_arrival(partial_sum, MP, 3) * gelu_slope(preact)
    weight_grad = adasum_columns(gradient / float(positions))
    return (output, input_grad, weight_grad)


def solution(mesh):
    split = Mesh(mesh.devices.reshape(4, 16, 4, 2), ("dp_0", "dp_1", "mp_0", "mp_1"))
    placed = (P(DP, None, None, MP), P(MP, None, None), P(DP, None, None, MP))
    return jax.shard_map(
        local,
        mesh=split,
        in_specs=placed,
        out_specs=(P(DP, None, None, MP), P(DP, None, None, MP), P(MP, DP)),
        check_vma=False,
    )
```

profile of v0, /device:TPU:1, one launch (start us, length us, event | category | flops | bytes accessed | tf_op | source)
XLA Modules:
  0.0 497.9 jit_solution(12086035207891262873)
XLA Ops:
  12.2 24.2 %all_to_all.75 = f32[8,1,16,16,128]{4,3,2,1,0:T(8,128)S(1)} all-to-all(f32[8,1,16,16,128]{4,3,2,1,0:T(8,128)S(1)} %bitcast.322), channel_id=1, replica_groups=mesh['dp_0'=4,'dp_1'=16,'mp_0'=4,'mp_1'=2] {'mp_0','mp_1'}, dimensions={0} | all-to-all | bytes 2097152 | tf_op jit(solution)/shard_map/all_to_all | solution.py:49
  38.9 18.6 %all_to_all.76 = f32[8,1,16,16,128]{4,3,2,1,0:T(8,128)S(1)} all-to-all(f32[8,1,16,16,128]{4,3,2,1,0:T(8,128)S(1)} %broadcast_in_dim.39), channel_id=1, replica_groups=mesh['dp_0'=4,'dp_1'=16,'mp_0'=4,'mp_1'=2] {'mp_0','mp_1'}, dimensions={0} | all-to-all | bytes 2097152 | tf_op jit(solution)/shard_map/all_to_all | solution.py:17
  59.1 2.5 reshape.545
  70.6 3.4 copy.94
  74.0 6.3 %div.108 = f32[64,64,144]{2,1,0:T(8,128)} reshape(f32[64,9,1024]{2,1,0:T(8,128)} %copy.94) | data formatting | bytes 4718592 | tf_op jit(solution)/shard_map/div | solution.py:146
  80.4 4.6 copy.95
  85.0 196.3 %all_to_all.77 = f32[64,64,144]{2,0,1:T(8,128)S(1)} all-to-all(f32[64,64,144]{2,0,1:T(8,128)S(1)} %copy.95), channel_id=1, replica_groups=mesh['dp_0'=4,'dp_1'=16,'mp_0'=4,'mp_1'=2] {'dp_0','dp_1'}, dimensions={1} | all-to-all | bytes 4718592 | tf_op jit(solution)/shard_map/all_to_all | solution.py:115
  281.3 2.5 multiply_reduce_fusion.2
  283.9 14.2 %all_to_all.78 = f32[8,32,3]{1,2,0:T(4,128)S(1)} all-to-all(f32[8,32,3]{1,2,0:T(4,128)S(1)} %broadcast_in_dim.40), channel_id=1, replica_groups=mesh['dp_0'=4,'dp_1'=16,'mp_0'=4,'mp_1'=2] {'mp_0','mp_1'}, dimensions={0} | all-to-all | bytes 6144 | tf_op jit(solution)/shard_map/all_to_all | solution.py:17
  298.1 21.3 %all_to_all.79 = f32[64,32,3]{1,2,0:T(4,128)S(1)} all-to-all(f32[64,32,3]{1,2,0:T(4,128)S(1)} %broadcast_in_dim.41), channel_id=1, replica_groups=mesh['dp_0'=4,'dp_1'=16,'mp_0'=4,'mp_1'=2] {'dp_0','dp_1'}, dimensions={0} | all-to-all | bytes 49152 | tf_op jit(solution)/shard_map/all_to_all | solution.py:17
  319.7 2.5 fusion
  323.9 10.0 %all_to_all.80 = f32[8,16,3]{1,2,0:T(4,128)S(1)} all-to-all(f32[8,16,3]{1,2,0:T(4,128)S(1)} %broadcast_in_dim.42), channel_id=1, replica_groups=mesh['dp_0'=4,'dp_1'=16,'mp_0'=4,'mp_1'=2] {'mp_0','mp_1'}, dimensions={0} | all-to-all | bytes 3072 | tf_op jit(solution)/shard_map/all_to_all | solution.py:17
  334.6 5.3 %all-to-all-start.6 = ((f32[64,16,3]{1,2,0:T(4,128)}), f32[64,16,3]{1,2,0:T(4,128)S(1)}, u32[]{:S(2)}, u32[]{:S(2)}) async-start(f32[64,16,3]{1,2,0:T(4,128)} %broadcast_in_dim.43), calls=%async_computation.6 | async-start | bytes 262144 | tf_op jit(solution)/shard_map/all_to_all | solution.py:17
  341.5 12.6 %all-to-all-done.6 = f32[64,16,3]{1,2,0:T(4,128)S(1)} async-done(((f32[64,16,3]{1,2,0:T(4,128)}), f32[64,16,3]{1,2,0:T(4,128)S(1)}, u32[]{:S(2)}, u32[]{:S(2)}) %all-to-all-start.6) | async-done | bytes 12320 | tf_op jit(solution)/shard_map/all_to_all | solution.py:17
  357.9 6.3 %all-to-all-start.7 = ((f32[8,8,3]{1,2,0:T(4,128)}), f32[8,8,3]{1,2,0:T(4,128)S(1)}, u32[]{:S(2)}, u32[]{:S(2)}) async-start(f32[8,8,3]{1,2,0:T(4,128)} %broadcast_in_dim.44), calls=%async_computation.7 | async-start | bytes 32768 | tf_op jit(solution)/shard_map/all_to_all | solution.py:17
  365.8 3.0 all-to-all-done.7
  369.6 5.8 %all-to-all-start.8 = ((f32[64,8,3]{1,2,0:T(4,128)}), f32[64,8,3]{1,2,0:T(4,128)}, u32[]{:S(2)}, u32[]{:S(2)}) async-start(f32[64,8,3]{1,2,0:T(4,128)} %broadcast_in_dim.45), calls=%async_computation.8 | async-start | bytes 262144 | tf_op jit(solution)/shard_map/all_to_all | solution.py:17
  377.3 12.1 %all-to-all-done.8 = f32[64,8,3]{1,2,0:T(4,128)} async-done(((f32[64,8,3]{1,2,0:T(4,128)}), f32[64,8,3]{1,2,0:T(4,128)}, u32[]{:S(2)}, u32[]{:S(2)}) %all-to-all-start.8) | async-done | bytes 6176 | tf_op jit(solution)/shard_map/all_to_all | solution.py:17
  393.3 6.4 %all-to-all-start.9 = ((f32[8,4,3]{1,2,0:T(4,128)}), f32[8,4,3]{1,2,0:T(4,128)S(1)}, u32[]{:S(2)}, u32[]{:S(2)}) async-start(f32[8,4,3]{1,2,0:T(4,128)} %broadcast_in_dim.46), calls=%async_computation.9 | async-start | bytes 32768 | tf_op jit(solution)/shard_map/all_to_all | solution.py:17
  401.4 3.0 all-to-all-done.9
  405.1 5.6 %all-to-all-start.10 = ((f32[64,4,3]{1,2,0:T(4,128)}), f32[64,4,3]{1,2,0:T(4,128)}, u32[]{:S(2)}, u32[]{:S(2)}) async-start(f32[64,4,3]{1,2,0:T(4,128)} %broadcast_in_dim.47), calls=%async_computation.10 | async-start | bytes 262144 | tf_op jit(solution)/shard_map/all_to_all | solution.py:17
  412.9 11.8 %all-to-all-done.10 = f32[64,4,3]{1,2,0:T(4,128)} async-done(((f32[64,4,3]{1,2,0:T(4,128)}), f32[64,4,3]{1,2,0:T(4,128)}, u32[]{:S(2)}, u32[]{:S(2)}) %all-to-all-start.10) | async-done | bytes 3104 | tf_op jit(solution)/shard_map/all_to_all | solution.py:17
  428.5 6.4 %all-to-all-start.11 = ((f32[8,2,3]{2,1,0:T(2,128)}), f32[8,2,3]{2,1,0:T(2,128)S(1)}, u32[]{:S(2)}, u32[]{:S(2)}) async-start(f32[8,2,3]{2,1,0:T(2,128)} %broadcast_in_dim.48), calls=%async_computation.11 | async-start | bytes 16384 | tf_op jit(solution)/shard_map/all_to_all | solution.py:17
  436.5 3.0 all-to-all-done.11
  440.2 5.3 %all-to-all-start.12 = ((f32[64,2,3]{2,1,0:T(2,128)}), f32[64,2,3]{2,1,0:T(2,128)S(1)}, u32[]{:S(2)}, u32[]{:S(2)}) async-start(f32[64,2,3]{2,1,0:T(2,128)} %broadcast_in_dim.49), calls=%async_computation.12 | async-start | bytes 131072 | tf_op jit(solution)/shard_map/all_to_all | solution.py:17
  445.5 2.5 convolution_add_fusion.10
  448.0 11.0 %all-to-all-done.12 = f32[64,2,3]{2,1,0:T(2,128)S(1)} async-done(((f32[64,2,3]{2,1,0:T(2,128)}), f32[64,2,3]{2,1,0:T(2,128)S(1)}, u32[]{:S(2)}, u32[]{:S(2)}) %all-to-all-start.12) | async-done | bytes 1568 | tf_op jit(solution)/shard_map/all_to_all | solution.py:17
  463.8 5.4 %all-to-all-start.13 = ((f32[8,1,3]{2,1,0:T(1,128)}), f32[8,1,3]{2,1,0:T(1,128)S(1)}, u32[]{:S(2)}, u32[]{:S(2)}) async-start(f32[8,1,3]{2,1,0:T(1,128)} %broadcast_in_dim.50), calls=%async_computation.13 | async-start | bytes 8192 | tf_op jit(solution)/shard_map/all_to_all | solution.py:17
  469.1 2.5 convolution_add_fusion.9
  474.3 5.4 %all-to-all-start.14 = ((f32[64,1,3]{2,1,0:T(1,128)}), f32[64,1,3]{2,1,0:T(1,128)}, u32[]{:S(2)}, u32[]{:S(2)}) async-start(f32[64,1,3]{2,1,0:T(1,128)} %broadcast_in_dim.51), calls=%async_computation.14 | async-start | bytes 65536 | tf_op jit(solution)/shard_map/all_to_all | solution.py:17
  479.8 2.5 fusion.10
  482.3 10.5 %all-to-all-done.14 = f32[64,1,3]{2,1,0:T(1,128)} async-done(((f32[64,1,3]{2,1,0:T(1,128)}), f32[64,1,3]{2,1,0:T(1,128)}, u32[]{:S(2)}, u32[]{:S(2)}) %all-to-all-start.14) | async-done | bytes 800 | tf_op jit(solution)/shard_map/all_to_all | solution.py:17
  (105 shorter events, 61.1 us)
Async XLA Ops:
  0.6 4.2 copy-start
  0.6 4.2 copy-start.1
  57.5 1.6 copy-start.3
  63.8 2.5 copy-start.2
  334.6 19.6 %all-to-all-start.6 = ((f32[64,16,3]{1,2,0:T(4,128)}), f32[64,16,3]{1,2,0:T(4,128)S(1)}, u32[]{:S(2)}, u32[]{:S(2)}) async-start(f32[64,16,3]{1,2,0:T(4,128)} %broadcast_in_dim.43), calls=%async_computation.6 | async-start | bytes 262144 | tf_op jit(solution)/shard_map/all_to_all | solution.py:17
  354.4 9.8 %copy-start.5 = (f32[16,16,64]{2,1,0:T(8,128)S(1)}, f32[16,16,64]{2,1,0:T(8,128)}, u32[]{:S(2)}) copy-start(f32[16,16,64]{2,1,0:T(8,128)} %fusion.35) | copy-start | bytes 196612
  357.9 10.9 %all-to-all-start.7 = ((f32[8,8,3]{1,2,0:T(4,128)}), f32[8,8,3]{1,2,0:T(4,128)S(1)}, u32[]{:S(2)}, u32[]{:S(2)}) async-start(f32[8,8,3]{1,2,0:T(4,128)} %broadcast_in_dim.44), calls=%async_computation.7 | async-start | bytes 32768 | tf_op jit(solution)/shard_map/all_to_all | solution.py:17
  369.6 19.8 %all-to-all-start.8 = ((f32[64,8,3]{1,2,0:T(4,128)}), f32[64,8,3]{1,2,0:T(4,128)}, u32[]{:S(2)}, u32[]{:S(2)}) async-start(f32[64,8,3]{1,2,0:T(4,128)} %broadcast_in_dim.45), calls=%async_computation.8 | async-start | bytes 262144 | tf_op jit(solution)/shard_map/all_to_all | solution.py:17
  393.3 11.1 %all-to-all-start.9 = ((f32[8,4,3]{1,2,0:T(4,128)}), f32[8,4,3]{1,2,0:T(4,128)S(1)}, u32[]{:S(2)}, u32[]{:S(2)}) async-start(f32[8,4,3]{1,2,0:T(4,128)} %broadcast_in_dim.46), calls=%async_computation.9 | async-start | bytes 32768 | tf_op jit(solution)/shard_map/all_to_all | solution.py:17
  405.1 19.5 %all-to-all-start.10 = ((f32[64,4,3]{1,2,0:T(4,128)}), f32[64,4,3]{1,2,0:T(4,128)}, u32[]{:S(2)}, u32[]{:S(2)}) async-start(f32[64,4,3]{1,2,0:T(4,128)} %broadcast_in_dim.47), calls=%async_computation.10 | async-start | bytes 262144 | tf_op jit(solution)/shard_map/all_to_all | solution.py:17
  426.9 0.7 copy-start.4
  428.5 11.0 %all-to-all-start.11 = ((f32[8,2,3]{2,1,0:T(2,128)}), f32[8,2,3]{2,1,0:T(2,128)S(1)}, u32[]{:S(2)}, u32[]{:S(2)}) async-start(f32[8,2,3]{2,1,0:T(2,128)} %broadcast_in_dim.48), calls=%async_computation.11 | async-start | bytes 16384 | tf_op jit(solution)/shard_map/all_to_all | solution.py:17
  440.2 18.8 %all-to-all-start.12 = ((f32[64,2,3]{2,1,0:T(2,128)}), f32[64,2,3]{2,1,0:T(2,128)S(1)}, u32[]{:S(2)}, u32[]{:S(2)}) async-start(f32[64,2,3]{2,1,0:T(2,128)} %broadcast_in_dim.49), calls=%async_computation.12 | async-start | bytes 131072 | tf_op jit(solution)/shard_map/all_to_all | solution.py:17
  463.8 9.9 %all-to-all-start.13 = ((f32[8,1,3]{2,1,0:T(1,128)}), f32[8,1,3]{2,1,0:T(1,128)S(1)}, u32[]{:S(2)}, u32[]{:S(2)}) async-start(f32[8,1,3]{2,1,0:T(1,128)} %broadcast_in_dim.50), calls=%async_computation.13 | async-start | bytes 8192 | tf_op jit(solution)/shard_map/all_to_all | solution.py:17
  474.3 18.5 %all-to-all-start.14 = ((f32[64,1,3]{2,1,0:T(1,128)}), f32[64,1,3]{2,1,0:T(1,128)}, u32[]{:S(2)}, u32[]{:S(2)}) async-start(f32[64,1,3]{2,1,0:T(1,128)} %broadcast_in_dim.51), calls=%async_computation.14 | async-start | bytes 65536 | tf_op jit(solution)/shard_map/all_to_all | solution.py:17
where the time goes:
time: 505 us; the launch traced here: 498 us
  blocking collectives  285 us (56%)
  waiting for transfers between devices  69.1 us (14%)
  starting transfers between devices  51.8 us (10%)
  matrix products  36.7 us (7%)
  local copies, waits for them, and re-layouts  28.4 us (6%)
  other arithmetic  23.5 us (5%)
    all_to_all x1, blocking collectives, adasum_columns(): spread = lax.all_to_all(blocks, DP, split_axis=1, concat_axis=1, tiled=True)  196 us
    all_to_all x9, waiting for transfers between devices, copy_for_each(): return lax.all_to_all(copies, axis, split_axis=0, concat_axis=0, tiled=True)  69.1 us
    all_to_all x4, blocking collectives, copy_for_each(): return lax.all_to_all(copies, axis, split_axis=0, concat_axis=0, tiled=True)  64 us
    all_to_all x9, starting transfers between devices, copy_for_each(): return lax.all_to_all(copies, axis, split_axis=0, concat_axis=0, tiled=True)  51.8 us
    all_to_all x1, blocking collectives, summed_on_arrival(): lax.all_to_all(parts, axis, split_axis=0, concat_axis=0, tiled=True)  24.2 us
    dot_general x9, matrix products, convolve_piece(): jnp.einsum('nhwc,oc->nhwo', window, filters[:, kernel_tap, :], precision=...  18.2 us
    div x3, local copies, waits for them, and re-layouts, local(): weight_grad = adasum_columns(gradient / float(positions))  14.4 us
    dot_general x9, matrix products, input_partial(): jnp.einsum('nhwo,oc->nhwc', window, filters[:, kernel_tap, :], precision=...  11.1 us
  transfers between devices with their start and end apart: 9, of which 9 were waited for; matrix products, arithmetic and copies ran while one was open for 4% of the time, Pallas kernels for 0%

commit v1 on v0

v1 whole, which is shorter than its diff:
```python
import functools

import jax
import jax.numpy as jnp
from jax import lax
from jax.experimental import pallas as pl
from jax.experimental.pallas import tpu as pltpu
from jax.sharding import PartitionSpec as P

MESH = pl.DeviceIdType.MESH
F32 = jnp.float32
BF16 = jnp.bfloat16
EPS = 1e-06
SIDE = 16
PIX = SIDE * SIDE
TAPS = 9
STACK = 640


def halves(values):
    high = values.astype(BF16)
    low = (values - high.astype(F32)).astype(BF16)
    return high, low


def dot3(a, b, dims):
    one = lambda p, q: lax.dot_general(p, q, (dims, ((), ())), preferred_element_type=F32)
    return one(a[0], b[0]) + (one(a[0], b[1]) + one(a[1], b[0]))


NN = ((1,), (0,))
NT = ((1,), (1,))


def shifted(values, dy, dx):
    pixel = lax.broadcasted_iota(jnp.int32, values.shape, 1)
    column = jnp.bitwise_and(pixel, SIDE - 1)
    inside = None
    if dx:
        inside = (column >= 1) if dx < 0 else (column < SIDE - 1)
    if dy:
        rows = (pixel >= SIDE) if dy < 0 else (pixel < PIX - SIDE)
        inside = rows if inside is None else jnp.logical_and(inside, rows)
    step = SIDE * dy + dx
    if step == 0:
        return values
    return jnp.where(inside, pltpu.roll(values, (-step) % PIX, 1), 0.0)


def stacked_taps(cot):
    taps = [shifted(cot, 1 - t // 3, 1 - t % 3) for t in range(TAPS)]
    return jnp.concatenate(taps + [jnp.zeros_like(cot)], axis=0)


def gram(ref, n, rows):
    total = None
    for r in range(rows // 8):
        block = halves(ref[:, 8 * r : 8 * r + 8, :].reshape(8 * n, STACK))
        part = dot3(block, block, NT)
        total = part if total is None else total + part
    sub = lax.broadcasted_iota(jnp.int32, total.shape, 0)
    lane = lax.broadcasted_iota(jnp.int32, total.shape, 1)
    kept = jnp.where(jnp.bitwise_and(sub, 7) == jnp.bitwise_and(lane, 7), total, 0.0)
    kept = jnp.sum(kept.reshape(n, 8, 8 * n), axis=1)
    source = lax.broadcasted_iota(jnp.int32, (8 * n, 128), 0)
    target = lax.broadcasted_iota(jnp.int32, (8 * n, 128), 1)
    fold = jnp.where(jnp.right_shift(source, 3) == target, 1.0, 0.0).astype(F32)
    return lax.dot_general(kept, fold, (NN, ((), ())), preferred_element_type=F32, precision=lax.Precision.HIGHEST)


def coefficients(table, n):
    rows = table.shape[0]
    sub = lax.broadcasted_iota(jnp.int32, table.shape, 0)
    lane = lax.broadcasted_iota(jnp.int32, table.shape, 1)
    diagonal = sub == lane
    result = jnp.ones((rows, 1), F32)
    b = 1
    while b < n:
        partner = jnp.bitwise_xor(sub, b) == lane
        own = jnp.where(diagonal, table, 0.0)
        cross = jnp.where(partner, table, 0.0)
        down = 1.0 - jnp.sum(cross, 1, keepdims=True) / (2.0 * (jnp.sum(own, 1, keepdims=True) + EPS))
        along = 1.0 - jnp.sum(cross, 0, keepdims=True) / (2.0 * (jnp.sum(own, 0, keepdims=True) + EPS))
        result = result * down
        if 2 * b < n:
            table = table * down * along
            moved = jnp.where(jnp.bitwise_and(sub, b) != 0, pltpu.roll(table, b, 0), pltpu.roll(table, rows - b, 0))
            table = table + moved
            moved = jnp.where(jnp.bitwise_and(lane, b) != 0, pltpu.roll(table, b, 1), pltpu.roll(table, 128 - b, 1))
            table = table + moved
        b *= 2
    return jnp.broadcast_to(result, (rows, 128))


def kernel(
    NY, NZ, NX,
    x_ref, cot_ref, w_hbm,
    out_ref, ig_ref, wg_ref,
    wv, wh, wl, ac, at, ct, ig, rp, rx, lt, cb, bt, yb, wf, ob, gm, gz, hm, hz, hy,
    wsem, za, cr, cl, acx, acp, atx, atp, rps, rxs, gms, gzs, ys, hms, hzs, hys, ps,
):
    NM = 2 * NX
    NDP = NY * NZ
    CD = x_ref.shape[1]
    CG = 8 * NM
    GROUPS = TAPS * NM // NY
    QUARTER = CG // NY
    dp = lax.axis_index("dp")
    me = lax.axis_index("mp")
    y, z = lax.div(dp, NZ), lax.rem(dp, NZ)
    x, c = lax.div(me, 2), lax.rem(me, 2)
    mate = me + 1 - 2 * c
    ring = lambda k: y * NZ + lax.rem(z + k + NZ, NZ)
    across = lambda k: 2 * lax.rem(x + k + NX, NX) + c

    def remote(src, dst, sems, k, r, to_dp, to_mp):
        return pltpu.make_async_remote_copy(
            src_ref=src, dst_ref=dst, send_sem=sems.at[0, k], recv_sem=sems.at[1, r],
            device_id=(to_dp, to_mp), device_id_type=MESH,
        )

    barrier = pltpu.get_barrier_semaphore()

    @pl.loop(1, NDP)
    def _(k):
        pl.semaphore_signal(barrier, inc=1, device_id=(lax.rem(dp + k, NDP), me), device_id_type=MESH)

    @pl.loop(1, NM)
    def _(k):
        pl.semaphore_signal(barrier, inc=1, device_id=(dp, lax.rem(me + k, NM)), device_id_type=MESH)

    weights_in = pltpu.make_async_copy(w_hbm, wv, wsem)
    weights_in.start()

    pre = x_ref[...]
    act = 0.5 * pre * (1.0 + lax.erf(pre * 0.7071067811865476))
    ac[me] = act.T
    at[me, z] = ac[me, pl.ds(pl.multiple_of(8 * z, 8), 8), :]
    cot = cot_ref[...]
    cot_t = jnp.concatenate([cot, jnp.zeros_like(cot)], axis=1).T[:64]
    ct[z] = cot_t

    weights_in.wait()
    for t in range(TAPS):
        high, low = halves(wv[:, t, :])
        wh[64 * t : 64 * t + 64, :] = high
        wl[64 * t : 64 * t + 64, :] = low
    wh[64 * TAPS :, :] = jnp.zeros_like(wh[64 * TAPS :, :])
    wl[64 * TAPS :, :] = jnp.zeros_like(wl[64 * TAPS :, :])

    stack_t = halves(stacked_taps(cot_t).T)
    for m in range(0, NM, 2):
        span = slice(CD * m, CD * m + 2 * CD)
        pair = dot3(stack_t, (wh[:, span], wl[:, span]), NN)
        ig[m] = pair[:, :CD]
        ig[m + 1] = pair[:, CD:]

    pl.semaphore_wait(barrier, NDP - 1 + NM - 1)

    def to_ring(k):
        there = lax.rem(z + k, NZ)
        rows = pl.ds(pl.multiple_of(8 * there, 8), 8)
        return remote(ac.at[me, rows], at.at[me, z], za, k, k, y * NZ + there, me)

    @pl.loop(1, NZ)
    def _(k):
        to_ring(k).start()

    def across_x(buf, sems, k):
        return remote(buf.at[me], buf.at[me], sems, k, k, dp, across(k))

    def to_mate(buf, sems, k):
        block = across(-k)
        return remote(buf.at[block], buf.at[block], sems, k, k, dp, mate)

    RIGHT, LEFT = NZ // 2, NZ // 2 - 1

    def rightward(s):
        image = lax.rem(z - s + 1 + NZ, NZ)
        return remote(ct.at[image], ct.at[image], cr, s, s, ring(1), me)

    def leftward(s):
        image = lax.rem(z + s - 1, NZ)
        return remote(ct.at[image], ct.at[image], cl, s, s, ring(-1), me)

    rightward(1).start()
    leftward(1).start()
    for k in range(1, NX):
        across_x(ac, acx, k).start()
    to_mate(ac, acp, 0).start()

    def mates_share(k):
        return remote(ig.at[2 * k + 1 - c], rp.at[k], rps, k, k, dp, mate)

    for k in range(NX):
        mates_share(k).start()

    def start_channels():
        @pl.loop(1, NZ)
        def _(k):
            to_ring(k).wait_recv()

        for k in range(1, NX):
            across_x(at, atx, k).start()
        to_mate(at, atp, 0).start()

    def pass_activations():
        for k in range(1, NX):
            across_x(ac, acx, k).wait_recv()
            to_mate(ac, acp, k).start()

    def share(k):
        own = across(k)
        return remote(ig.at[own], rx.at[x], rxs, k, k, dp, own)

    def start_shares():
        for k in range(NX):
            mates_share(k).wait_recv()
            ig[2 * k + c] = ig[2 * k + c] + rp[k]
        for k in range(1, NX):
            share(k).start()

    def pass_channels():
        for k in range(1, NX):
            across_x(at, atx, k).wait_recv()
            to_mate(at, atp, k).start()

    def channels_here():
        for k in range(NX):
            to_mate(at, atp, k).wait_recv()

    def leaf(image):
        stack = halves(stacked_taps(ct[image]))
        channels = halves(at[:, image].reshape(CG, PIX))
        lt[image] = dot3(channels, stack, NT) * (1.0 / PIX)

    def leaves_until(first, last):
        def work():
            @pl.loop(first, last)
            def _(j):
                half = lax.div(j + 1, 2)
                side = 1 - 2 * lax.rem(j, 2)
                leaf(lax.rem(z + side * half + NZ, NZ))
        return work

    items = [
        (1, pass_activations),
        (2, start_channels),
        (3, start_shares),
        (4, pass_channels),
        (5, channels_here),
        (5, leaves_until(0, min(7, NZ))),
    ]
    if NZ == 16:
        items += [(6, leaves_until(7, 11)), (7, leaves_until(11, 15)), (8, leaves_until(15, 16))]

    for s in range(1, RIGHT + 1):
        rightward(s).wait_recv()
        if s < RIGHT:
            rightward(s + 1).start()
        if s <= LEFT:
            leftward(s).wait_recv()
            if s < LEFT:
                leftward(s + 1).start()
        while items and (items[0][0] <= s or s == RIGHT):
            items.pop(0)[1]()

    def exchange(buf, n, mine, sems, device, between=None):
        there = lambda k: lax.rem(mine + k, n)

        @pl.loop(1, n)
        def _(k):
            remote(buf.at[mine], buf.at[mine], sems, k, k, *device(there(k))).start()

        if between is not None:
            between()

        @pl.loop(1, n)
        def _(k):
            remote(buf.at[mine], buf.at[there(n - k)], sems, k, k, *device(there(k))).wait_recv()

        total = buf[0]
        for k in range(1, n):
            total = total + buf[k]
        return total

    def sent(n, buf, mine, sems, device):
        there = lambda k: lax.rem(mine + k, n)

        @pl.loop(1, n)
        def _(k):
            remote(buf.at[mine], buf.at[mine], sems, k, k, *device(there(k))).wait_send()

    on_mp = lambda k: (dp, k)
    on_z = lambda k: (y * NZ + k, me)
    on_y = lambda k: (k * NZ + z, me)

    def convolve():
        for k in range(NX):
            to_mate(ac, acp, k).wait_recv()
        full = halves(ac[...].reshape(NM * CD, PIX))
        total = None
        for t in range(TAPS):
            rows = slice(64 * t, 64 * t + 64)
            product = dot3((wh[rows, :], wl[rows, :]), full, NN)
            moved = shifted(product, t // 3 - 1, t % 3 - 1)
            total = moved if total is None else total + moved
        out_ref[...] = total

    def finish_shares():
        total = ig[me]
        for k in range(1, NX):
            share(k).wait_recv()
            total = total + rx[lax.rem(x - k + NX, NX)]
        ig_ref[...] = total

    table = gram(lt, NZ, CG)
    lane = lax.broadcasted_iota(jnp.int32, (8, 128), 1)
    if NZ == 16:
        gm[me] = jnp.where(lane < 16, table[:8], pltpu.roll(table[8:], 16, 1))
    else:
        gm[me] = jnp.concatenate([table, jnp.zeros((8 - NZ, 128), F32)], axis=0)
    gz[z] = exchange(gm, NM, me, gms, on_mp)
    table = exchange(gz, NZ, z, gzs, on_z, convolve)
    if NZ == 16:
        table = jnp.concatenate([table, pltpu.roll(table, 112, 1)], axis=0)
    rows = table.shape[0]
    cb[0:rows, :] = coefficients(table, NZ)
    total = None
    for i in range(NZ):
        scale = jnp.concatenate([cb[i : i + 1, :]] * (STACK // 128), axis=1)
        term = lt[i] * scale
        total = term if total is None else total + term
    bt[...] = total
    yb[y] = bt[pl.ds(pl.multiple_of(QUARTER * y, 8), QUARTER), :]

    def to_y(k):
        there = lax.rem(y + k, NY)
        rows = pl.ds(pl.multiple_of(QUARTER * there, 8), QUARTER)
        return remote(bt.at[rows], yb.at[y], ys, k, k, there * NZ + z, me)

    for k in range(1, NY):
        to_y(k).start()
    finish_shares()
    for k in range(1, NY):
        to_y(k).wait_recv()
    table = gram(yb, NY, QUARTER)
    hm[me] = jnp.concatenate([table, jnp.zeros((8 - NY, 128), F32)], axis=0)
    hy[y] = exchange(hm, NM, me, hms, on_mp)
    hz[z] = exchange(hy, NY, y, hys, on_y)
    table = exchange(hz, NZ, z, hzs, on_z)
    cb[0:8, :] = coefficients(table, NY)
    total = None
    for i in range(NY):
        scale = jnp.concatenate([cb[i : i + 1, :]] * (STACK // 128), axis=1)
        term = yb[i] * scale
        total = term if total is None else total + term
    wf[...] = total

    def group(j):
        m, tap = divmod(j, TAPS)
        number = NZ * NM * tap + NZ * ((QUARTER // 8) * y + m) + z
        owner, slot = lax.div(number, GROUPS), lax.rem(number, GROUPS)
        source = wf.at[pl.ds(8 * m, 8), pl.ds(128 * (tap // 2), 128)]
        return owner, slot, source

    for j in range(GROUPS):
        owner, slot, source = group(j)

        @pl.when(owner != dp)
        def _():
            remote(source, ob.at[slot], ps, j, slot, owner, me).start()

        @pl.when(owner == dp)
        def _():
            pltpu.make_async_copy(source, ob.at[slot], ps.at[1, slot]).start()

    for s in range(GROUPS):
        pltpu.make_async_copy(ob.at[s], ob.at[s], ps.at[1, s]).wait()
        tap = lax.div(GROUPS * dp + s, NZ * NM)
        piece = ob[s]
        wg_ref[8 * s : 8 * s + 8, :] = jnp.where(lax.rem(tap, 2) == 1, pltpu.roll(piece, 64, 1), piece)

    @pl.loop(1, NZ)
    def _(k):
        to_ring(k).wait_send()

    for s in range(1, RIGHT + 1):
        rightward(s).wait_send()
    for s in range(1, LEFT + 1):
        leftward(s).wait_send()
    for k in range(NX):
        if k:
            across_x(ac, acx, k).wait_send()
            across_x(at, atx, k).wait_send()
            share(k).wait_send()
        to_mate(ac, acp, k).wait_send()
        to_mate(at, atp, k).wait_send()
        mates_share(k).wait_send()
    for k in range(1, NY):
        to_y(k).wait_send()
    sent(NM, gm, me, gms, on_mp)
    sent(NZ, gz, z, gzs, on_z)
    sent(NM, hm, me, hms, on_mp)
    sent(NZ, hz, z, hzs, on_z)
    sent(NY, hy, y, hys, on_y)
    for j in range(GROUPS):
        owner, slot, source = group(j)

        @pl.when(owner != dp)
        def _():
            remote(source, ob.at[slot], ps, j, slot, owner, me).wait_send()


def gelu_slope(values):
    return (
        0.5 * (1.0 + lax.erf(values * 0.7071067811865476))
        + values * jnp.exp(-0.5 * values * values) * 0.3989422804014327
    )


def local(NY, NZ, NX, preact, weights, cotangent):
    NM = 2 * NX
    CD = preact.shape[3]
    CG = 8 * NM
    QUARTER = CG // NY
    GROUPS = TAPS * NM // NY
    vmem = lambda *shape: pltpu.VMEM(shape, F32)
    sems = lambda n: pltpu.SemaphoreType.DMA((2, n))
    whole = pl.BlockSpec(memory_space=pltpu.VMEM)
    pre = preact.reshape(PIX, CD)
    out, ig, wg = pl.pallas_call(
        functools.partial(kernel, NY, NZ, NX),
        out_shape=(
            jax.ShapeDtypeStruct((64, PIX), F32),
            jax.ShapeDtypeStruct((PIX, CD), F32),
            jax.ShapeDtypeStruct((8 * GROUPS, 128), F32),
        ),
        in_specs=[whole, whole, pl.BlockSpec(memory_space=pl.ANY)],
        out_specs=(whole, whole, whole),
        scratch_shapes=[
            vmem(*weights.shape),
            pltpu.VMEM((STACK, NM * CD), BF16),
            pltpu.VMEM((STACK, NM * CD), BF16),
            vmem(NM, CD, PIX),
            vmem(NM, NZ, 8, PIX),
            vmem(NZ, 64, PIX),
            vmem(NM, PIX, CD),
            vmem(NX, PIX, CD),
            vmem(NX, PIX, CD),
            vmem(NZ, CG, STACK),
            vmem(16, 128),
            vmem(CG, STACK),
            vmem(NY, QUARTER, STACK),
            vmem(QUARTER, STACK),
            vmem(GROUPS, 8, 128),
            vmem(NM, 8, 128),
            vmem(NZ, 8, 128),
            vmem(NM, 8, 128),
            vmem(NZ, 8, 128),
            vmem(NY, 8, 128),
            pltpu.SemaphoreType.DMA,
            sems(NZ), sems(NZ), sems(NZ),
            sems(NX), sems(NX), sems(NX), sems(NX), sems(NX), sems(NX),
            sems(NM), sems(NZ), sems(NY), sems(NM), sems(NZ), sems(NY),
            sems(GROUPS),
        ],
        compiler_params=pltpu.CompilerParams(collective_id=0, has_side_effects=True),
        name="step",
    )(pre, cotangent.reshape(PIX, 64), weights)
    output = out.T.reshape(1, SIDE, SIDE, 64)
    input_grad = (ig * gelu_slope(pre)).reshape(preact.shape)
    return output, input_grad, wg[:, :64].T


def build(mesh, NY, NZ, NX):
    placed = (P("dp", None, None, "mp"), P("mp", None, None), P("dp", None, None, "mp"))
    return jax.shard_map(
        functools.partial(local, NY, NZ, NX),
        mesh=mesh,
        in_specs=placed,
        out_specs=(P("dp", None, None, "mp"), P("dp", None, None, "mp"), P("mp", "dp")),
        check_vma=False,
    )


def solution(mesh):
    return build(mesh, 4, mesh.shape["dp"] // 4, mesh.shape["mp"] // 2)
```

time: 505 us -> 116 us (0.23)
  blocking collectives: 285 us -> 0 us
  Pallas kernels: 0 us -> 103 us
  waiting for transfers between devices: 69.1 us -> 0 us
  starting transfers between devices: 51.8 us -> 0 us
  matrix products: 36.7 us -> 0 us
  other arithmetic: 23.5 us -> 1.62 us
  local copies, waits for them, and re-layouts: 28.4 us -> 8.34 us
    all_to_all x6 -> x0, blocking collectives: 285 us -> none  [the longest x1 196 us: adasum_columns(): spread = lax.all_to_all(blocks, DP, split_axis=1, concat_axis=1, tiled=True)]
    pallas_call x0 -> x1, Pallas kernels: none -> 103 us  [local(): pl.pallas_call(functools.partial(kernel, NY, NZ, NX), out_shape=(jax.Shap...]
    all_to_all x9 -> x0, waiting for transfers between devices: 69.1 us -> none  [copy_for_each(): return lax.all_to_all(copies, axis, split_axis=0, concat_axis=0, tiled=True)]
    all_to_all x9 -> x0, starting transfers between devices: 51.8 us -> none  [copy_for_each(): return lax.all_to_all(copies, axis, split_axis=0, concat_axis=0, tiled=True)]
    dot_general x27 -> x0, matrix products: 36.7 us -> none  [the longest x9 18.2 us: convolve_piece(): jnp.einsum('nhwc,oc->nhwo', window, filters[:, kernel_tap, :], precision=...]
    div x3 -> x0, local copies, waits for them, and re-layouts: 14.4 us -> none  [local(): weight_grad = adasum_columns(gradient / float(positions))]
    reduce_sum x20 -> x0, other arithmetic: 10.9 us -> none  [the longest x6 6.94 us: adasum_columns(): jnp.sum(leading * second, (0, 2))]
    add x6 -> x0, other arithmetic: 8.47 us -> none  [adasum_columns(): (1.0 - cross / (2.0 * (lead_sq + epsilon))) * leading]
  transfers between devices with their start and end apart: 9 -> 0, of which waited for: 9 -> 0; matrix products, arithmetic and copies ran while one was open for 4% -> 0% of each run, Pallas kernels for 0% -> 0%
where the time goes in v1:
time: 116 us; the launch traced here: 114 us
  Pallas kernels  103 us (89%)
  local copies, waits for them, and re-layouts  8.34 us (7%)
  other arithmetic  1.62 us (1%)
    pallas_call x1, Pallas kernels, local(): pl.pallas_call(functools.partial(kernel, NY, NZ, NX), out_shape=(jax.Shap...  103 us
    unnamed x4, local copies, waits for them, and re-layouts  5.86 us

profile of v1, /device:TPU:1, one launch (start us, length us, event | category | flops | bytes accessed | tf_op | source)
XLA Modules:
  0.0 113.6 jit_solution(2009799016472026699)
XLA Ops:
  0.6 0.0 copy-start
  0.6 5.1 %copy.9.w_hbm = f32[64,9,1024]{2,1,0:T(8,128)} copy(f32[64,9,1024]{2,0,1:T(8,128)} %param.4) | data formatting | bytes 4718592 | tf_op args[1]
  5.8 103.0 %step.1 = (f32[64,256]{1,0:T(8,128)}, f32[256,128]{1,0:T(8,128)}, f32[144,128]{1,0:T(8,128)}) custom-call(f32[256,128]{1,0:T(8,128)} %bitcast.8, f32[256,64]{1,0:T(8,128)} %bitcast.9, f32[64,9,1024]{2,1,0:T(8,128)} %copy.9.w_hbm), custom_call_target="tpu_custom_call" | custom-call | tf_op jit(solution)/shard_map/step/pallas_call | solution.py:432
  108.8 1.6 %copy.10 = f32[256,64]{1,0:T(8,128)} copy(f32[256,64]{0,1:T(8,128)} %bitcast.12) | data formatting | bytes 131072 | tf_op jit(solution)/shard_map/transpose | solution.py:471
  110.4 0.9 slice_bitcast_fusion
  111.3 0.7 copy.11
  112.0 0.0 copy-done
  112.0 1.6 %fusion.4 = f32[256,128]{1,0:T(8,128)} fusion(f32[256,128]{1,0:T(8,128)} %get-tuple-element.7, f32[1,16,16,128]{3,2,1,0:T(8,128)S(1)} %copy-done), kind=kLoop, calls=%fused_computation.5 | loop fusion | flops 294912 | bytes 393216 | tf_op jit(solution)/shard_map/mul | solution.py:472
Async XLA Ops:
  0.6 111.4 %copy-start = (f32[1,16,16,128]{3,2,1,0:T(8,128)S(1)}, f32[1,16,16,128]{3,2,1,0:T(8,128)}, u32[]{:S(2)}) copy-start(f32[1,16,16,128]{3,2,1,0:T(8,128)} %param.3) | copy-start | bytes 393220

commit v2 on v1

v2 whole, which is shorter than its diff:
```python
import functools

import jax
import jax.numpy as jnp
from jax import lax
from jax.experimental import pallas as pl
from jax.experimental.pallas import tpu as pltpu
from jax.sharding import PartitionSpec as P

MESH = pl.DeviceIdType.MESH
F32 = jnp.float32
BF16 = jnp.bfloat16
EPS = 1e-06
SIDE = 16
PIX = SIDE * SIDE
TAPS = 9
STACK = 640


def halves(values):
    high = values.astype(BF16)
    low = (values - high.astype(F32)).astype(BF16)
    return high, low


def dot3(a, b, dims):
    one = lambda p, q: lax.dot_general(p, q, (dims, ((), ())), preferred_element_type=F32)
    return one(a[0], b[0]) + (one(a[0], b[1]) + one(a[1], b[0]))


NN = ((1,), (0,))
NT = ((1,), (1,))


def shifted(values, dy, dx):
    pixel = lax.broadcasted_iota(jnp.int32, values.shape, 1)
    column = jnp.bitwise_and(pixel, SIDE - 1)
    inside = None
    if dx:
        inside = (column >= 1) if dx < 0 else (column < SIDE - 1)
    if dy:
        rows = (pixel >= SIDE) if dy < 0 else (pixel < PIX - SIDE)
        inside = rows if inside is None else jnp.logical_and(inside, rows)
    step = SIDE * dy + dx
    if step == 0:
        return values
    return jnp.where(inside, pltpu.roll(values, (-step) % PIX, 1), 0.0)


def stacked_taps(cot):
    taps = [shifted(cot, 1 - t // 3, 1 - t % 3) for t in range(TAPS)]
    return jnp.concatenate(taps + [jnp.zeros_like(cot)], axis=0)


def gram(ref, n, rows):
    total = None
    for r in range(rows // 8):
        block = halves(ref[:, 8 * r : 8 * r + 8, :].reshape(8 * n, STACK))
        part = dot3(block, block, NT)
        total = part if total is None else total + part
    sub = lax.broadcasted_iota(jnp.int32, total.shape, 0)
    lane = lax.broadcasted_iota(jnp.int32, total.shape, 1)
    kept = jnp.where(jnp.bitwise_and(sub, 7) == jnp.bitwise_and(lane, 7), total, 0.0)
    kept = jnp.sum(kept.reshape(n, 8, 8 * n), axis=1)
    source = lax.broadcasted_iota(jnp.int32, (8 * n, 128), 0)
    target = lax.broadcasted_iota(jnp.int32, (8 * n, 128), 1)
    fold = jnp.where(jnp.right_shift(source, 3) == target, 1.0, 0.0).astype(F32)
    return lax.dot_general(kept, fold, (NN, ((), ())), preferred_element_type=F32, precision=lax.Precision.HIGHEST)


def packed(table, n):
    per = min(n, 128 // n)
    rows = []
    for r in range(n // per):
        row = table[r * per : r * per + 1]
        for i in range(1, per):
            row = row + pltpu.roll(table[r * per + i : r * per + i + 1], n * i, 1)
        rows.append(row)
    return rows[0] if len(rows) == 1 else jnp.concatenate(rows, axis=0)


def unpacked(rows, n, scratch):
    per = min(n, 128 // n)
    held = max(n, 8)
    if n < 8:
        scratch[0:8, :] = jnp.zeros((8, 128), F32)
    for i in range(n):
        row = rows[i // per : i // per + 1]
        scratch[i : i + 1, :] = pltpu.roll(row, (128 - n * (i % per)) % 128, 1) if i % per else row
    return scratch[0:held, :]


def coefficients(table, n):
    rows = table.shape[0]
    sub = lax.broadcasted_iota(jnp.int32, table.shape, 0)
    lane = lax.broadcasted_iota(jnp.int32, table.shape, 1)
    diagonal = sub == lane
    result = jnp.ones((rows, 1), F32)
    b = 1
    while b < n:
        partner = jnp.bitwise_xor(sub, b) == lane
        own = jnp.where(diagonal, table, 0.0)
        cross = jnp.where(partner, table, 0.0)
        down = 1.0 - jnp.sum(cross, 1, keepdims=True) / (2.0 * (jnp.sum(own, 1, keepdims=True) + EPS))
        along = 1.0 - jnp.sum(cross, 0, keepdims=True) / (2.0 * (jnp.sum(own, 0, keepdims=True) + EPS))
        result = result * down
        if 2 * b < n:
            table = table * down * along
            moved = jnp.where(jnp.bitwise_and(sub, b) != 0, pltpu.roll(table, b, 0), pltpu.roll(table, rows - b, 0))
            table = table + moved
            moved = jnp.where(jnp.bitwise_and(lane, b) != 0, pltpu.roll(table, b, 1), pltpu.roll(table, 128 - b, 1))
            table = table + moved
        b *= 2
    return jnp.broadcast_to(result, (rows, 128))


def gelu_slope(values):
    return (
        0.5 * (1.0 + lax.erf(values * 0.7071067811865476))
        + values * jnp.exp(-0.5 * values * values) * 0.3989422804014327
    )


CHUNKS = 2


def kernel(
    NY, NZ, NX,
    x_ref, cot_ref, w_hbm,
    out_ref, ig_ref, wg_ref,
    wv, wh, wl, ac, at, ct, ig, rp, rx, lt, cb, bt, yb, pk, ob, gm, gz, hm, hz,
    wsem, za, cr, cl, acx, acp, atx, atp, rps, rxs, gms, gzs, ys, hms, hzs, ps,
):
    NM = 2 * NX
    CD = x_ref.shape[1]
    CG = 8 * NM
    GROUPS = TAPS * NM // NY
    QUARTER = CG // NY
    HALF = NZ // 2
    dp = lax.axis_index("dp")
    me = lax.axis_index("mp")
    y, z = lax.div(dp, NZ), lax.rem(dp, NZ)
    x, c = lax.div(me, 2), lax.rem(me, 2)
    mate = me + 1 - 2 * c
    ring = lambda k: y * NZ + lax.rem(z + k + NZ, NZ)
    across = lambda k: 2 * lax.rem(x + k + NX, NX) + c

    def remote(src, dst, sems, k, r, to_dp, to_mp):
        return pltpu.make_async_remote_copy(
            src_ref=src, dst_ref=dst, send_sem=sems.at[0, k], recv_sem=sems.at[1, r],
            device_id=(to_dp, to_mp), device_id_type=MESH,
        )

    with jax.named_scope("signals"):
        barrier = pltpu.get_barrier_semaphore()

        @pl.loop(1, NZ)
        def _(k):
            pl.semaphore_signal(barrier, inc=1, device_id=(ring(k), me), device_id_type=MESH)

        for k in range(1, NY):
            pl.semaphore_signal(barrier, inc=1, device_id=(lax.rem(y + k, NY) * NZ + z, me), device_id_type=MESH)
        for k in range(1, NM):
            pl.semaphore_signal(barrier, inc=1, device_id=(dp, lax.rem(me + k, NM)), device_id_type=MESH)

    weights_in = pltpu.make_async_copy(w_hbm, wv, wsem)
    weights_in.start()

    with jax.named_scope("gelu"):
        pre = x_ref[...]
        act = 0.5 * pre * (1.0 + lax.erf(pre * 0.7071067811865476))
        ac[me] = act.T
        at[me, 0] = ac[me, pl.ds(pl.multiple_of(8 * z, 8), 8), :]
        cot = cot_ref[...]
        cot_t = jnp.concatenate([cot, jnp.zeros_like(cot)], axis=1).T[:64]
        ct[z] = cot_t

    with jax.named_scope("wprep"):
        weights_in.wait()
        for t in range(TAPS):
            high, low = halves(wv[t])
            wh[64 * t : 64 * t + 64, :] = high
            wl[64 * t : 64 * t + 64, :] = low
        wh[64 * TAPS :, :] = jnp.zeros_like(wh[64 * TAPS :, :])
        wl[64 * TAPS :, :] = jnp.zeros_like(wl[64 * TAPS :, :])

    with jax.named_scope("igpart"):
        stack_t = halves(stacked_taps(cot_t).T)
        for m in range(0, NM, 2):
            span = slice(CD * m, CD * m + 2 * CD)
            pair = dot3(stack_t, (wh[:, span], wl[:, span]), NN)
            ig[m] = pair[:, :CD]
            ig[m + 1] = pair[:, CD:]

    with jax.named_scope("barwait"):
        pl.semaphore_wait(barrier, NZ - 1 + NY - 1 + NM - 1)

    def offset(j):
        half = lax.div(j + 1, 2)
        return half * (2 * lax.rem(j, 2) - 1)

    def to_ring(j):
        there = lax.rem(z + offset(j) + NZ, NZ)
        rows = pl.ds(pl.multiple_of(8 * there, 8), 8)
        return remote(ac.at[me, rows], at.at[me, j], za, j, j, y * NZ + there, me)

    def across_x(k):
        return remote(ac.at[me], ac.at[me], acx, k, k, dp, across(k))

    def to_mate(k):
        block = across(-k)
        return remote(ac.at[block], ac.at[block], acp, k, k, dp, mate)

    def part_across_x(p, k):
        part = at.at[me, pl.ds(HALF * p, HALF)]
        return remote(part, part, atx, NX * p + k, NX * p + k, dp, across(k))

    def part_to_mate(p, k):
        part = at.at[across(-k), pl.ds(HALF * p, HALF)]
        return remote(part, part, atp, NX * p + k, NX * p + k, dp, mate)

    RIGHT, LEFT = NZ // 2, NZ // 2 - 1
    TALL = 64 // CHUNKS

    def rightward(s, q):
        part = ct.at[lax.rem(z - s + 1 + NZ, NZ), pl.ds(TALL * q, TALL)]
        return remote(part, part, cr, CHUNKS * s + q, CHUNKS * s + q, ring(1), me)

    def leftward(s, q):
        part = ct.at[lax.rem(z + s - 1, NZ), pl.ds(TALL * q, TALL)]
        return remote(part, part, cl, CHUNKS * s + q, CHUNKS * s + q, ring(-1), me)

    for q in range(CHUNKS):
        rightward(1, q).start()
        leftward(1, q).start()

    @pl.loop(1, NZ)
    def _(j):
        to_ring(j).start()

    def mates_share(k):
        return remote(ig.at[2 * k + 1 - c], rp.at[k], rps, k, k, dp, mate)

    for k in range(NX):
        mates_share(k).start()

    def start_part(p):
        @pl.loop(max(1, HALF * p), HALF * (p + 1))
        def _(j):
            to_ring(j).wait_recv()

        for k in range(1, NX):
            part_across_x(p, k).start()
        part_to_mate(p, 0).start()

    def pass_part(p):
        for k in range(1, NX):
            part_across_x(p, k).wait_recv()
            part_to_mate(p, k).start()

    def part_here(p):
        for k in range(NX):
            part_to_mate(p, k).wait_recv()

    def start_activations():
        for k in range(1, NX):
            across_x(k).start()
        to_mate(0).start()

    def pass_activations():
        for k in range(1, NX):
            across_x(k).wait_recv()
            to_mate(k).start()

    def share(k):
        own = across(k)
        return remote(ig.at[own], rx.at[x], rxs, k, k, dp, own)

    def add_shares():
        for k in range(NX):
            mates_share(k).wait_recv()
            ig[2 * k + c] = ig[2 * k + c] + rp[k]

    def start_shares():
        for k in range(1, NX):
            share(k).start()

    def leaves(first, last):
        @pl.loop(first, last)
        def _(j):
            image = lax.rem(z - offset(j) + NZ, NZ)
            stack = halves(stacked_taps(ct[image]))
            channels = halves(at[:, j].reshape(CG, PIX))
            lt[image] = dot3(channels, stack, NT) * (1.0 / PIX)

    if NZ == 16:
        plan = {
            (2, 0): [(start_part, 0)],
            (3, 0): [(add_shares,)],
            (4, 0): [(start_part, 1), (start_activations,), (start_shares,)],
            (5, 0): [(pass_part, 0)],
            (6, 0): [(part_here, 0), (leaves, 0, 4)],
            (6, 1): [(leaves, 4, 8)],
            (7, 1): [(pass_part, 1)],
            (8, 1): [(part_here, 1), (leaves, 8, 16)],
        }
    else:
        plan = {
            (RIGHT, 1): [
                (start_part, 0), (add_shares,), (start_part, 1), (start_activations,), (start_shares,),
                (pass_part, 0), (part_here, 0), (pass_part, 1), (part_here, 1), (leaves, 0, NZ),
            ],
        }

    for s in range(1, RIGHT + 1):
        for q in range(CHUNKS):
            with jax.named_scope(f"wait{s}_{q}"):
                rightward(s, q).wait_recv()
                if s < RIGHT:
                    rightward(s + 1, q).start()
                if s <= LEFT:
                    leftward(s, q).wait_recv()
                    if s < LEFT:
                        leftward(s + 1, q).start()
            for work in plan.get((s, q), []):
                with jax.named_scope(f"{work[0].__name__}{work[1] if len(work) > 1 else 0}"):
                    work[0](*work[1:])

    def exchange(buf, n, mine, sems, device, between=None):
        there = lambda k: lax.rem(mine + k, n)

        @pl.loop(1, n)
        def _(k):
            remote(buf.at[mine], buf.at[mine], sems, k, k, *device(there(k))).start()

        if between is not None:
            between()

        @pl.loop(1, n)
        def _(k):
            remote(buf.at[mine], buf.at[there(n - k)], sems, k, k, *device(there(k))).wait_recv()

        total = buf[0]
        for k in range(1, n):
            total = total + buf[k]
        return total

    def sent(n, buf, mine, sems, device):
        there = lambda k: lax.rem(mine + k, n)

        @pl.loop(1, n)
        def _(k):
            remote(buf.at[mine], buf.at[mine], sems, k, k, *device(there(k))).wait_send()

    on_mp = lambda k: (dp, k)
    on_z = lambda k: (y * NZ + k, me)
    on_y_mp = lambda k: (lax.div(k, NM) * NZ + z, lax.rem(k, NM))

    def convolve():
        for k in range(NX):
            to_mate(k).wait_recv()
        full = halves(ac[...].reshape(NM * CD, PIX))
        total = None
        for t in range(TAPS):
            rows = slice(64 * t, 64 * t + 64)
            product = dot3((wh[rows, :], wl[rows, :]), full, NN)
            moved = shifted(product, t // 3 - 1, t % 3 - 1)
            total = moved if total is None else total + moved
        total = jnp.concatenate([total, jnp.zeros_like(total)], axis=0).T
        out_ref[...] = total[:, :64]

    def finish_shares():
        total = ig[me]
        for k in range(1, NX):
            share(k).wait_recv()
            total = total + rx[lax.rem(x - k + NX, NX)]
        ig_ref[...] = total * gelu_slope(x_ref[...])

    with jax.named_scope("gram16"):
        gm[me] = packed(gram(lt, NZ, CG), NZ)
    with jax.named_scope("g16mp"):
        gz[z] = exchange(gm, NM, me, gms, on_mp, pass_activations)
    with jax.named_scope("g16z"):
        table = exchange(gz, NZ, z, gzs, on_z, convolve)
    with jax.named_scope("coef16"):
        table = unpacked(table, NZ, cb)
        rows = table.shape[0]
        cb[0:rows, :] = coefficients(table, NZ)
    with jax.named_scope("comb16"):
        total = None
        for i in range(NZ):
            scale = jnp.concatenate([cb[i : i + 1, :]] * (STACK // 128), axis=1)
            term = lt[i] * scale
            total = term if total is None else total + term
        bt[...] = total
        yb[y] = bt[pl.ds(pl.multiple_of(QUARTER * y, 8), QUARTER), :]

    def to_y(k):
        there = lax.rem(y + k, NY)
        rows = pl.ds(pl.multiple_of(QUARTER * there, 8), QUARTER)
        return remote(bt.at[rows], yb.at[y], ys, k, k, there * NZ + z, me)

    with jax.named_scope("ywait"):
        for k in range(1, NY):
            to_y(k).start()
        for k in range(1, NY):
            to_y(k).wait_recv()

    def group(j):
        m, tap = divmod(j, TAPS)
        number = NZ * NM * tap + NZ * ((QUARTER // 8) * y + m) + z
        return lax.div(number, GROUPS), lax.rem(number, GROUPS)

    lower = lax.broadcasted_iota(jnp.int32, (8, 128), 1) < 64

    def send_groups():
        with jax.named_scope("permsend"):
            for j in range(GROUPS):
                m, tap = divmod(j, TAPS)
                span = slice(128 * (tap // 2), 128 * (tap // 2) + 128)
                for h in range(NY // 2):
                    left = yb[2 * h, 8 * m : 8 * m + 8, span]
                    right = yb[2 * h + 1, 8 * m : 8 * m + 8, span]
                    if tap % 2:
                        left = pltpu.roll(left, 64, 1)
                    else:
                        right = pltpu.roll(right, 64, 1)
                    pk[j, 8 * h : 8 * h + 8, :] = jnp.where(lower, left, right)
            for j in range(GROUPS):
                owner, slot = group(j)

                @pl.when(owner != dp)
                def _():
                    remote(pk.at[j], ob.at[slot], ps, j, slot, owner, me).start()

                @pl.when(owner == dp)
                def _():
                    pltpu.make_async_copy(pk.at[j], ob.at[slot], ps.at[1, slot]).start()

    def settle():
        finish_shares()

        @pl.loop(1, NZ)
        def _(j):
            to_ring(j).wait_send()

        for q in range(CHUNKS):
            for s in range(1, RIGHT + 1):
                rightward(s, q).wait_send()
            for s in range(1, LEFT + 1):
                leftward(s, q).wait_send()
        for k in range(NX):
            if k:
                across_x(k).wait_send()
                share(k).wait_send()
                for p in range(2):
                    part_across_x(p, k).wait_send()
            to_mate(k).wait_send()
            mates_share(k).wait_send()
            for p in range(2):
                part_to_mate(p, k).wait_send()
        for k in range(1, NY):
            to_y(k).wait_send()
        sent(NM, gm, me, gms, on_mp)
        sent(NZ, gz, z, gzs, on_z)

    with jax.named_scope("gram4"):
        here = NM * y + me
        hm[here] = packed(gram(yb, NY, QUARTER), NY)
    with jax.named_scope("g4ymp"):
        hz[z] = exchange(hm, NY * NM, here, hms, on_y_mp, send_groups)
    with jax.named_scope("g4z"):
        table = exchange(hz, NZ, z, hzs, on_z, settle)
    with jax.named_scope("coef4"):
        table = unpacked(table, NY, cb)
        cb[0:8, :] = coefficients(table, NY)
        scales = [jnp.where(lower, cb[2 * h : 2 * h + 1, :], cb[2 * h + 1 : 2 * h + 2, :]) for h in range(NY // 2)]
    with jax.named_scope("permrecv"):
        pieces = []
        for s in range(GROUPS):
            pltpu.make_async_copy(ob.at[s], ob.at[s], ps.at[1, s]).wait()
            piece = None
            for h in range(NY // 2):
                term = ob[s, 8 * h : 8 * h + 8, :] * scales[h]
                piece = term if piece is None else piece + term
            pieces.append(piece)
        columns = jnp.concatenate(pieces, axis=0)
        columns = columns + pltpu.roll(columns, 64, 1)
        fill = -8 * GROUPS % 128
        columns = jnp.concatenate([columns, jnp.zeros((fill, 128), F32)], axis=0).T
        wg_ref[...] = columns[:64, : 8 * GROUPS]

    with jax.named_scope("drain"):
        sent(NY * NM, hm, here, hms, on_y_mp)
        sent(NZ, hz, z, hzs, on_z)
        for j in range(GROUPS):
            owner, slot = group(j)

            @pl.when(owner != dp)
            def _():
                remote(pk.at[j], ob.at[slot], ps, j, slot, owner, me).wait_send()


def local(NY, NZ, NX, preact, weights, cotangent):
    NM = 2 * NX
    CD = preact.shape[3]
    CG = 8 * NM
    QUARTER = CG // NY
    GROUPS = TAPS * NM // NY
    rows16 = NZ // min(NZ, 128 // NZ)
    vmem = lambda *shape: pltpu.VMEM(shape, F32)
    sems = lambda n: pltpu.SemaphoreType.DMA((2, n))
    whole = pl.BlockSpec(memory_space=pltpu.VMEM)
    output, input_grad, weight_grad = pl.pallas_call(
        functools.partial(kernel, NY, NZ, NX),
        out_shape=(
            jax.ShapeDtypeStruct((PIX, 64), F32),
            jax.ShapeDtypeStruct((PIX, CD), F32),
            jax.ShapeDtypeStruct((64, 8 * GROUPS), F32),
        ),
        in_specs=[whole, whole, pl.BlockSpec(memory_space=pl.ANY)],
        out_specs=(whole, whole, whole),
        scratch_shapes=[
            vmem(TAPS, 64, NM * CD),
            pltpu.VMEM((STACK, NM * CD), BF16),
            pltpu.VMEM((STACK, NM * CD), BF16),
            vmem(NM, CD, PIX),
            vmem(NM, NZ, 8, PIX),
            vmem(NZ, 64, PIX),
            vmem(NM, PIX, CD),
            vmem(NX, PIX, CD),
            vmem(NX, PIX, CD),
            vmem(NZ, CG, STACK),
            vmem(16, 128),
            vmem(CG, STACK),
            vmem(NY, QUARTER, STACK),
            vmem(GROUPS, 4 * NY, 128),
            vmem(GROUPS, 4 * NY, 128),
            vmem(NM, rows16, 128),
            vmem(NZ, rows16, 128),
            vmem(NY * NM, 1, 128),
            vmem(NZ, 1, 128),
            pltpu.SemaphoreType.DMA,
            sems(NZ), sems(CHUNKS * NZ), sems(CHUNKS * NZ),
            sems(NX), sems(NX), sems(2 * NX), sems(2 * NX), sems(NX), sems(NX),
            sems(NM), sems(NZ), sems(NY), sems(NY * NM), sems(NZ),
            sems(GROUPS),
        ],
        compiler_params=pltpu.CompilerParams(collective_id=0, has_side_effects=True),
        name="step",
    )(preact.reshape(PIX, CD), cotangent.reshape(PIX, 64), weights.transpose(1, 0, 2))
    return output.reshape(1, SIDE, SIDE, 64), input_grad.reshape(preact.shape), weight_grad


def build(mesh, NY, NZ, NX):
    placed = (P("dp", None, None, "mp"), P("mp", None, None), P("dp", None, None, "mp"))
    return jax.shard_map(
        functools.partial(local, NY, NZ, NX),
        mesh=mesh,
        in_specs=placed,
        out_specs=(P("dp", None, None, "mp"), P("dp", None, None, "mp"), P("mp", "dp")),
        check_vma=False,
    )


def solution(mesh):
    return build(mesh, 4, mesh.shape["dp"] // 4, mesh.shape["mp"] // 2)
```

time: 116 us -> 92.8 us (0.80); the launches traced: 114 us -> 92.5 us
  Pallas kernels: 103 us -> 87.3 us
  local copies, waits for them, and re-layouts: 8.34 us -> 4.61 us
  other arithmetic: 1.62 us -> 0 us
    pallas_call x1, Pallas kernels: 103 us -> 87.3 us  [local(): pl.pallas_call(functools.partial(kernel, NY, NZ, NX), out_shape=(jax.Shap...]
    transpose x2 -> x0, local copies, waits for them, and re-layouts: 2.48 us -> none  [the longest x1 1.59 us: local(): output = out.T.reshape(1, SIDE, SIDE, 64)]
    mul x1 -> x0, other arithmetic: 1.62 us -> none  [local(): input_grad = (ig * gelu_slope(pre)).reshape(preact.shape)]
    unnamed x4 -> x3, local copies, waits for them, and re-layouts: 5.86 us -> 4.61 us
where the time goes in v2:
time: 92.8 us; the launch traced here: 92.5 us
  Pallas kernels  87.3 us (94%)
  local copies, waits for them, and re-layouts  4.61 us (5%)
    pallas_call x1, Pallas kernels, local(): pl.pallas_call(functools.partial(kernel, NY, NZ, NX), out_shape=(jax.Shap...  87.3 us
    unnamed x3, local copies, waits for them, and re-layouts  4.61 us

profile of v2, /device:TPU:1, one launch (start us, length us, event | category | flops | bytes accessed | tf_op | source)
XLA Modules:
  0.0 92.5 jit_solution(10282791387488433623)
XLA Ops:
  0.6 87.3 %step.1 = (f32[256,64]{1,0:T(8,128)}, f32[256,128]{1,0:T(8,128)}, f32[64,144]{1,0:T(8,128)}) custom-call(f32[256,128]{1,0:T(8,128)} %bitcast.6, f32[256,64]{1,0:T(8,128)} %bitcast.7, f32[9,64,1024]{2,1,0:T(8,128)} %bitcast.5), custom_call_target="tpu_custom_call" | custom-call | tf_op jit(solution)/shard_map/step/pallas_call | solution.py:514
  87.9 1.6 %copy.9 = f32[1,16,16,64]{3,2,1,0:T(8,128)} copy(f32[1,16,16,64]{3,2,1,0:T(8,128)} %bitcast.9) | data formatting | bytes 131072
  89.5 1.6 %copy.10 = f32[1,16,16,128]{3,2,1,0:T(8,128)} copy(f32[1,16,16,128]{3,2,1,0:T(8,128)} %bitcast.8) | data formatting | bytes 262144
  91.1 1.5 %copy.11 = f32[64,144]{1,0:T(8,128)} copy(f32[64,144]{1,0:T(8,128)} %get-tuple-element.14) | data formatting | bytes 73728

commit v3 on v2

--- a/solution.py
+++ b/solution.py
@@ -26,6 +26,13 @@
 def dot3(a, b, dims):
     one = lambda p, q: lax.dot_general(p, q, (dims, ((), ())), preferred_element_type=F32)
     return one(a[0], b[0]) + (one(a[0], b[1]) + one(a[1], b[0]))
+
+
+def dot3_joined(a, b, dims):
+    one = lambda p, q: lax.dot_general(p, q, (dims, ((), ())), preferred_element_type=F32)
+    rows = a[0].shape[0]
+    both = one(jnp.concatenate(a, axis=0), b[0])
+    return both[:rows] + (both[rows:] + one(a[0], b[1]))
 
 
 NN = ((1,), (0,))
@@ -52,20 +59,27 @@
     return jnp.concatenate(taps + [jnp.zeros_like(cot)], axis=0)
 
 
+def folded(total, n, bits):
+    size = 1 << bits
+    sub = lax.broadcasted_iota(jnp.int32, total.shape, 0)
+    lane = lax.broadcasted_iota(jnp.int32, total.shape, 1)
+    kept = jnp.where(jnp.bitwise_and(sub, size - 1) == jnp.bitwise_and(lane, size - 1), total, 0.0)
+    kept = jnp.sum(kept.reshape(n, size, size * n), axis=1)
+    source = lax.broadcasted_iota(jnp.int32, (size * n, 128), 0)
+    target = lax.broadcasted_iota(jnp.int32, (size * n, 128), 1)
+    fold = jnp.where(jnp.right_shift(source, bits) == target, 1.0, 0.0).astype(F32)
+    return lax.dot_general(kept, fold, (NN, ((), ())), preferred_element_type=F32, precision=lax.Precision.HIGHEST)
+
+
 def gram(ref, n, rows):
     total = None
     for r in range(rows // 8):
         block = halves(ref[:, 8 * r : 8 * r + 8, :].reshape(8 * n, STACK))
-        part = dot3(block, block, NT)
+        both = jnp.concatenate(block, axis=0)
+        part = lax.dot_general(both, block[0], (NT, ((), ())), preferred_element_type=F32)
         total = part if total is None else total + part
-    sub = lax.broadcasted_iota(jnp.int32, total.shape, 0)
-    lane = lax.broadcasted_iota(jnp.int32, total.shape, 1)
-    kept = jnp.where(jnp.bitwise_and(sub, 7) == jnp.bitwise_and(lane, 7), total, 0.0)
-    kept = jnp.sum(kept.reshape(n, 8, 8 * n), axis=1)
-    source = lax.broadcasted_iota(jnp.int32, (8 * n, 128), 0)
-    target = lax.broadcasted_iota(jnp.int32, (8 * n, 128), 1)
-    fold = jnp.where(jnp.right_shift(source, 3) == target, 1.0, 0.0).astype(F32)
-    return lax.dot_general(kept, fold, (NN, ((), ())), preferred_element_type=F32, precision=lax.Precision.HIGHEST)
+    low = total[8 * n :]
+    return folded(total[: 8 * n] + (low + low.T), n, 3)
 
 
 def packed(table, n):
@@ -121,15 +135,15 @@
     )
 
 
-CHUNKS = 2
+CHUNKS = 4
 
 
 def kernel(
     NY, NZ, NX,
-    x_ref, cot_ref, w_hbm,
-    out_ref, ig_ref, wg_ref,
-    wv, wh, wl, ac, at, ct, ig, rp, rx, lt, cb, bt, yb, pk, ob, gm, gz, hm, hz,
-    wsem, za, cr, cl, acx, acp, atx, atp, rps, rxs, gms, gzs, ys, hms, hzs, ps,
+    x_hbm, cot_hbm, w_hbm,
+    out_hbm, ig_hbm, wg_hbm,
+    x_ref, cot_ref, out_ref, ig_ref, wg_ref, wv, wh, wl, ac, at, ct, ig, rp, rx, sh, sl, lt, cb, bt, yb, pk, ob, gm, gz, hm, hz,
+    isem, osem, za, cr, cl, acx, acp, atx, atp, rps, rxs, gms, gzs, ys, hms, hzs, ps,
 ):
     NM = 2 * NX
     CD = x_ref.shape[1]
@@ -151,6 +165,12 @@
             device_id=(to_dp, to_mp), device_id_type=MESH,
         )
 
+    x_in = pltpu.make_async_copy(x_hbm, x_ref, isem.at[0])
+    cot_in = pltpu.make_async_copy(cot_hbm, cot_ref, isem.at[1])
+    weights_in = pltpu.make_async_copy(w_hbm, wv, isem.at[2])
+    x_in.start()
+    cot_in.start()
+
     with jax.named_scope("signals"):
         barrier = pltpu.get_barrier_semaphore()
 
@@ -163,10 +183,11 @@
         for k in range(1, NM):
             pl.semaphore_signal(barrier, inc=1, device_id=(dp, lax.rem(me + k, NM)), device_id_type=MESH)
 
-    weights_in = pltpu.make_async_copy(w_hbm, wv, wsem)
     weights_in.start()
 
     with jax.named_scope("gelu"):
+        x_in.wait()
+        cot_in.wait()
         pre = x_ref[...]
         act = 0.5 * pre * (1.0 + lax.erf(pre * 0.7071067811865476))
         ac[me] = act.T
@@ -175,7 +196,59 @@
         cot_t = jnp.concatenate([cot, jnp.zeros_like(cot)], axis=1).T[:64]
         ct[z] = cot_t
 
-    with jax.named_scope("wprep"):
+    with jax.named_scope("barwait"):
+        pl.semaphore_wait(barrier, NZ - 1 + NY - 1 + NM - 1)
+
+    def offset(j):
+        half = lax.div(j + 1, 2)
+        return half * (2 * lax.rem(j, 2) - 1)
+
+    def to_ring(j):
+        there = lax.rem(z + offset(j) + NZ, NZ)
+        rows = pl.ds(pl.multiple_of(8 * there, 8), 8)
+        return remote(ac.at[me, rows], at.at[me, j], za, j, j, y * NZ + there, me)
+
+    def across_x(k):
+        return remote(ac.at[me], ac.at[me], acx, k, k, dp, across(k))
+
+    def to_mate(k):
+        block = across(-k)
+        return remote(ac.at[block], ac.at[block], acp, k, k, dp, mate)
+
+    def part_across_x(p, k):
+        part = at.at[me, pl.ds(HALF * p, HALF)]
+        return remote(part, part, atx, NX * p + k, NX * p + k, dp, across(k))
+
+    def part_to_mate(p, k):
+        part = at.at[across(-k), pl.ds(HALF * p, HALF)]
+        return remote(part, part, atp, NX * p + k, NX * p + k, dp, mate)
+
+    RIGHT, LEFT = NZ // 2, NZ // 2 - 1
+    TALL = 64 // CHUNKS
+
+    def rightward(s, q):
+        part = ct.at[lax.rem(z - s + 1 + NZ, NZ), pl.ds(TALL * q, TALL)]
+        return remote(part, part, cr, CHUNKS * s + q, CHUNKS * s + q, ring(1), me)
+
+    def leftward(s, q):
+        part = ct.at[lax.rem(z + s - 1, NZ), pl.ds(TALL * q, TALL)]
+        return remote(part, part, cl, CHUNKS * s + q, CHUNKS * s + q, ring(-1), me)
+
+    for q in range(CHUNKS):
+        rightward(1, q).start()
+        leftward(1, q).start()
+
+    def send_channels(first, end):
+        @pl.loop(first, end)
+        def _(j):
+            to_ring(j).start()
+
+    send_channels(1, HALF)
+
+    def mates_share(k):
+        return remote(ig.at[2 * k + 1 - c], rp.at[k], rps, k, k, dp, mate)
+
+    def prepare_weights():
         weights_in.wait()
         for t in range(TAPS):
             high, low = halves(wv[t])
@@ -184,65 +257,15 @@
         wh[64 * TAPS :, :] = jnp.zeros_like(wh[64 * TAPS :, :])
         wl[64 * TAPS :, :] = jnp.zeros_like(wl[64 * TAPS :, :])
 
-    with jax.named_scope("igpart"):
-        stack_t = halves(stacked_taps(cot_t).T)
+    def partial_sums():
+        stack_t = halves(stacked_taps(ct[z]).T)
         for m in range(0, NM, 2):
             span = slice(CD * m, CD * m + 2 * CD)
             pair = dot3(stack_t, (wh[:, span], wl[:, span]), NN)
             ig[m] = pair[:, :CD]
             ig[m + 1] = pair[:, CD:]
-
-    with jax.named_scope("barwait"):
-        pl.semaphore_wait(barrier, NZ - 1 + NY - 1 + NM - 1)
-
-    def offset(j):
-        half = lax.div(j + 1, 2)
-        return half * (2 * lax.rem(j, 2) - 1)
-
-    def to_ring(j):
-        there = lax.rem(z + offset(j) + NZ, NZ)
-        rows = pl.ds(pl.multiple_of(8 * there, 8), 8)
-        return remote(ac.at[me, rows], at.at[me, j], za, j, j, y * NZ + there, me)
-
-    def across_x(k):
-        return remote(ac.at[me], ac.at[me], acx, k, k, dp, across(k))
-
-    def to_mate(k):
-        block = across(-k)
-        return remote(ac.at[block], ac.at[block], acp, k, k, dp, mate)
-
-    def part_across_x(p, k):
-        part = at.at[me, pl.ds(HALF * p, HALF)]
-        return remote(part, part, atx, NX * p + k, NX * p + k, dp, across(k))
-
-    def part_to_mate(p, k):
-        part = at.at[across(-k), pl.ds(HALF * p, HALF)]
-        return remote(part, part, atp, NX * p + k, NX * p + k, dp, mate)
-
-    RIGHT, LEFT = NZ // 2, NZ // 2 - 1
-    TALL = 64 // CHUNKS
-
-    def rightward(s, q):
-        part = ct.at[lax.rem(z - s + 1 + NZ, NZ), pl.ds(TALL * q, TALL)]
-        return remote(part, part, cr, CHUNKS * s + q, CHUNKS * s + q, ring(1), me)
-
-    def leftward(s, q):
-        part = ct.at[lax.rem(z + s - 1, NZ), pl.ds(TALL * q, TALL)]
-        return remote(part, part, cl, CHUNKS * s + q, CHUNKS * s + q, ring(-1), me)
-
-    for q in range(CHUNKS):
-        rightward(1, q).start()
-        leftward(1, q).start()
-
-    @pl.loop(1, NZ)
-    def _(j):
-        to_ring(j).start()
-
-    def mates_share(k):
-        return remote(ig.at[2 * k + 1 - c], rp.at[k], rps, k, k, dp, mate)
-
-    for k in range(NX):
-        mates_share(k).start()
+        for k in range(NX):
+            mates_share(k).start()
 
     def start_part(p):
         @pl.loop(max(1, HALF * p), HALF * (p + 1))
@@ -285,30 +308,38 @@
         for k in range(1, NX):
             share(k).start()
 
-    def leaves(first, last):
-        @pl.loop(first, last)
+    def stacks(first, end):
+        @pl.loop(first, end)
         def _(j):
-            image = lax.rem(z - offset(j) + NZ, NZ)
-            stack = halves(stacked_taps(ct[image]))
+            sh[j], sl[j] = halves(stacked_taps(ct[lax.rem(z - offset(j) + NZ, NZ)]))
+
+    def leaves(first, end):
+        @pl.loop(first, end)
+        def _(j):
             channels = halves(at[:, j].reshape(CG, PIX))
-            lt[image] = dot3(channels, stack, NT) * (1.0 / PIX)
-
+            lt[lax.rem(z - offset(j) + NZ, NZ)] = dot3_joined(channels, (sh[j], sl[j]), NT) * (1.0 / PIX)
+
+    last = CHUNKS - 1
     if NZ == 16:
         plan = {
+            (1, 1): [(send_channels, HALF, NZ)],
+            (1, last): [(prepare_weights,), (stacks, 0, 1)],
             (2, 0): [(start_part, 0)],
-            (3, 0): [(add_shares,)],
-            (4, 0): [(start_part, 1), (start_activations,), (start_shares,)],
-            (5, 0): [(pass_part, 0)],
-            (6, 0): [(part_here, 0), (leaves, 0, 4)],
-            (6, 1): [(leaves, 4, 8)],
-            (7, 1): [(pass_part, 1)],
-            (8, 1): [(part_here, 1), (leaves, 8, 16)],
+            (2, last): [(stacks, 1, 3)],
+            (3, last): [(partial_sums,)],
+            (4, 0): [(start_part, 1), (stacks, 3, 5)],
+            (4, last): [(pass_part, 0), (stacks, 5, 7)],
+            (5, last): [(part_here, 0), (leaves, 0, 5), (add_shares,), (start_activations,), (start_shares,)],
+            (6, last): [(pass_part, 1), (leaves, 5, 7), (stacks, 7, 11), (leaves, 7, 8)],
+            (7, last): [(part_here, 1), (leaves, 8, 11), (stacks, 11, 15), (leaves, 11, 15)],
+            (8, last): [(stacks, 15, 16), (leaves, 15, 16)],
         }
     else:
         plan = {
-            (RIGHT, 1): [
+            (RIGHT, last): [
+                (send_channels, HALF, NZ), (prepare_weights,), (partial_sums,),
                 (start_part, 0), (add_shares,), (start_part, 1), (start_activations,), (start_shares,),
-                (pass_part, 0), (part_here, 0), (pass_part, 1), (part_here, 1), (leaves, 0, NZ),
+                (pass_part, 0), (part_here, 0), (pass_part, 1), (part_here, 1), (stacks, 0, NZ), (leaves, 0, NZ),
             ],
         }
 
@@ -356,6 +387,8 @@
     on_z = lambda k: (y * NZ + k, me)
     on_y_mp = lambda k: (lax.div(k, NM) * NZ + z, lax.rem(k, NM))
 
+    leave = lambda src, dst, k: pltpu.make_async_copy(src, dst, osem.at[k])
+
     def convolve():
         for k in range(NX):
             to_mate(k).wait_recv()
@@ -368,6 +401,7 @@
             total = moved if total is None else total + moved
         total = jnp.concatenate([total, jnp.zeros_like(total)], axis=0).T
         out_ref[...] = total[:, :64]
+        leave(out_ref, out_hbm, 0).start()
 
     def finish_shares():
         total = ig[me]
@@ -375,6 +409,7 @@
             share(k).wait_recv()
             total = total + rx[lax.rem(x - k + NX, NX)]
         ig_ref[...] = total * gelu_slope(x_ref[...])
+        leave(ig_ref, ig_hbm, 1).start()
 
     with jax.named_scope("gram16"):
         gm[me] = packed(gram(lt, NZ, CG), NZ)
@@ -489,8 +524,12 @@
         fill = -8 * GROUPS % 128
         columns = jnp.concatenate([columns, jnp.zeros((fill, 128), F32)], axis=0).T
         wg_ref[...] = columns[:64, : 8 * GROUPS]
+        leave(wg_ref, wg_hbm, 2).start()
 
     with jax.named_scope("drain"):
+        leave(out_ref, out_hbm, 0).wait()
+        leave(ig_ref, ig_hbm, 1).wait()
+        leave(wg_ref, wg_hbm, 2).wait()
         sent(NY * NM, hm, here, hms, on_y_mp)
         sent(NZ, hz, z, hzs, on_z)
         for j in range(GROUPS):
@@ -510,17 +549,22 @@
     rows16 = NZ // min(NZ, 128 // NZ)
     vmem = lambda *shape: pltpu.VMEM(shape, F32)
     sems = lambda n: pltpu.SemaphoreType.DMA((2, n))
-    whole = pl.BlockSpec(memory_space=pltpu.VMEM)
+    anywhere = pl.BlockSpec(memory_space=pl.ANY)
     output, input_grad, weight_grad = pl.pallas_call(
         functools.partial(kernel, NY, NZ, NX),
-        out_shape=(
+        out_shape=[
             jax.ShapeDtypeStruct((PIX, 64), F32),
             jax.ShapeDtypeStruct((PIX, CD), F32),
             jax.ShapeDtypeStruct((64, 8 * GROUPS), F32),
-        ),
-        in_specs=[whole, whole, pl.BlockSpec(memory_space=pl.ANY)],
-        out_specs=(whole, whole, whole),
+        ],
+        in_specs=[anywhere] * 3,
+        out_specs=[anywhere] * 3,
         scratch_shapes=[
+            vmem(PIX, CD),
+            vmem(PIX, 64),
+            vmem(PIX, 64),
+            vmem(PIX, CD),
+            vmem(64, 8 * GROUPS),
             vmem(TAPS, 64, NM * CD),
             pltpu.VMEM((STACK, NM * CD), BF16),
             pltpu.VMEM((STACK, NM * CD), BF16),
@@ -530,6 +574,8 @@
             vmem(NM, PIX, CD),
             vmem(NX, PIX, CD),
             vmem(NX, PIX, CD),
+            pltpu.VMEM((NZ, STACK, PIX), BF16),
+            pltpu.VMEM((NZ, STACK, PIX), BF16),
             vmem(NZ, CG, STACK),
             vmem(16, 128),
             vmem(CG, STACK),
@@ -540,7 +586,8 @@
             vmem(NZ, rows16, 128),
             vmem(NY * NM, 1, 128),
             vmem(NZ, 1, 128),
-            pltpu.SemaphoreType.DMA,
+            pltpu.SemaphoreType.DMA((3,)),
+            pltpu.SemaphoreType.DMA((3,)),
             sems(NZ), sems(CHUNKS * NZ), sems(CHUNKS * NZ),
             sems(NX), sems(NX), sems(2 * NX), sems(2 * NX), sems(NX), sems(NX),
             sems(NM), sems(NZ), sems(NY), sems(NY * NM), sems(NZ),
@@ -549,6 +596,19 @@
         compiler_params=pltpu.CompilerParams(collective_id=0, has_side_effects=True),
         name="step",
     )(preact.reshape(PIX, CD), cotangent.reshape(PIX, 64), weights.transpose(1, 0, 2))
+    def hand_over(a, b, d, e, f, g):
+        e[...] = a[...]
+        f[...] = b[...]
+        g[...] = d[...]
+
+    whole = pl.BlockSpec(memory_space=pltpu.VMEM)
+    output, input_grad, weight_grad = pl.pallas_call(
+        hand_over,
+        out_shape=[jax.ShapeDtypeStruct(v.shape, F32) for v in (output, input_grad, weight_grad)],
+        in_specs=[whole] * 3,
+        out_specs=[whole] * 3,
+        name="hand_over",
+    )(output, input_grad, weight_grad)
     return output.reshape(1, SIDE, SIDE, 64), input_grad.reshape(preact.shape), weight_grad
 
 

time: 92.8 us -> 83.9 us (0.904)
  local copies, waits for them, and re-layouts: 4.61 us -> 0 us
  Pallas kernels: 87.3 us -> 83.1 us
    unnamed x3 -> x0, local copies, waits for them, and re-layouts: 4.61 us -> none
    pallas_call x1 -> x2, Pallas kernels: 87.3 us -> 83.1 us  [the longest x1 81.4 us: local(): pl.pallas_call(functools.partial(kernel, NY, NZ, NX), out_shape=[jax.Shap...]
where the time goes in v3:
time: 83.9 us; the launch traced here: 83.7 us
  Pallas kernels  83.1 us (99%)
    pallas_call x1, Pallas kernels, local(): pl.pallas_call(functools.partial(kernel, NY, NZ, NX), out_shape=[jax.Shap...  81.4 us
    pallas_call x1, Pallas kernels, local(): pl.pallas_call(hand_over, out_shape=[jax.ShapeDtypeStruct(v.shape, F32) f...  1.7 us

profile of v3, /device:TPU:1, one launch (start us, length us, event | category | flops | bytes accessed | tf_op | source)
XLA Modules:
  0.0 83.7 jit_solution(1528035904508482414)
XLA Ops:
  0.6 81.4 %step.1 = (f32[256,64]{1,0:T(8,128)}, f32[256,128]{1,0:T(8,128)}, f32[64,144]{1,0:T(8,128)}) custom-call(f32[256,128]{1,0:T(8,128)} %bitcast.6, f32[256,64]{1,0:T(8,128)} %bitcast.7, f32[9,64,1024]{2,1,0:T(8,128)} %bitcast.5), custom_call_target="tpu_custom_call" | custom-call | tf_op jit(solution)/shard_map/step/pallas_call | solution.py:553
  82.0 1.7 %hand_over.1 = (f32[256,64]{1,0:T(8,128)}, f32[256,128]{1,0:T(8,128)}, f32[64,144]{1,0:T(8,128)}) custom-call(f32[256,64]{1,0:T(8,128)} %get-tuple-element.9.a, f32[256,128]{1,0:T(8,128)} %get-tuple-element.10.b, f32[64,144]{1,0:T(8,128)} %get-tuple-element.11.d), custom_call_target="tpu_custom_call" | custom-call | tf_op jit(solution)/shard_map/hand_over/pallas_call | solution.py:605

commit v4 on v3

--- a/solution.py
+++ b/solution.py
@@ -135,15 +135,16 @@
     )
 
 
-CHUNKS = 4
+CHUNKS = 2
+LIMIT = 54500 * 1024
 
 
 def kernel(
     NY, NZ, NX,
     x_hbm, cot_hbm, w_hbm,
-    out_hbm, ig_hbm, wg_hbm,
-    x_ref, cot_ref, out_ref, ig_ref, wg_ref, wv, wh, wl, ac, at, ct, ig, rp, rx, sh, sl, lt, cb, bt, yb, pk, ob, gm, gz, hm, hz,
-    isem, osem, za, cr, cl, acx, acp, atx, atp, rps, rxs, gms, gzs, ys, hms, hzs, ps,
+    out_ref, ig_ref, wg_ref,
+    x_ref, cot_ref, wv, wh, wl, ac, at, ct, ig, rp, rx, sh, sl, lt, cb, bt, yb, pk, ob, gm, gz, hm, hz,
+    isem, za, cr, cl, acx, acp, atx, atp, rps, rxs, gms, gzs, ys, hms, hzs, ps,
 ):
     NM = 2 * NX
     CD = x_ref.shape[1]
@@ -196,59 +197,7 @@
         cot_t = jnp.concatenate([cot, jnp.zeros_like(cot)], axis=1).T[:64]
         ct[z] = cot_t
 
-    with jax.named_scope("barwait"):
-        pl.semaphore_wait(barrier, NZ - 1 + NY - 1 + NM - 1)
-
-    def offset(j):
-        half = lax.div(j + 1, 2)
-        return half * (2 * lax.rem(j, 2) - 1)
-
-    def to_ring(j):
-        there = lax.rem(z + offset(j) + NZ, NZ)
-        rows = pl.ds(pl.multiple_of(8 * there, 8), 8)
-        return remote(ac.at[me, rows], at.at[me, j], za, j, j, y * NZ + there, me)
-
-    def across_x(k):
-        return remote(ac.at[me], ac.at[me], acx, k, k, dp, across(k))
-
-    def to_mate(k):
-        block = across(-k)
-        return remote(ac.at[block], ac.at[block], acp, k, k, dp, mate)
-
-    def part_across_x(p, k):
-        part = at.at[me, pl.ds(HALF * p, HALF)]
-        return remote(part, part, atx, NX * p + k, NX * p + k, dp, across(k))
-
-    def part_to_mate(p, k):
-        part = at.at[across(-k), pl.ds(HALF * p, HALF)]
-        return remote(part, part, atp, NX * p + k, NX * p + k, dp, mate)
-
-    RIGHT, LEFT = NZ // 2, NZ // 2 - 1
-    TALL = 64 // CHUNKS
-
-    def rightward(s, q):
-        part = ct.at[lax.rem(z - s + 1 + NZ, NZ), pl.ds(TALL * q, TALL)]
-        return remote(part, part, cr, CHUNKS * s + q, CHUNKS * s + q, ring(1), me)
-
-    def leftward(s, q):
-        part = ct.at[lax.rem(z + s - 1, NZ), pl.ds(TALL * q, TALL)]
-        return remote(part, part, cl, CHUNKS * s + q, CHUNKS * s + q, ring(-1), me)
-
-    for q in range(CHUNKS):
-        rightward(1, q).start()
-        leftward(1, q).start()
-
-    def send_channels(first, end):
-        @pl.loop(first, end)
-        def _(j):
-            to_ring(j).start()
-
-    send_channels(1, HALF)
-
-    def mates_share(k):
-        return remote(ig.at[2 * k + 1 - c], rp.at[k], rps, k, k, dp, mate)
-
-    def prepare_weights():
+    with jax.named_scope("prepare"):
         weights_in.wait()
         for t in range(TAPS):
             high, low = halves(wv[t])
@@ -256,16 +205,69 @@
             wl[64 * t : 64 * t + 64, :] = low
         wh[64 * TAPS :, :] = jnp.zeros_like(wh[64 * TAPS :, :])
         wl[64 * TAPS :, :] = jnp.zeros_like(wl[64 * TAPS :, :])
-
-    def partial_sums():
-        stack_t = halves(stacked_taps(ct[z]).T)
+        stack = stacked_taps(cot_t)
+        sh[0], sl[0] = halves(stack)
+        stack_t = halves(stack.T)
         for m in range(0, NM, 2):
             span = slice(CD * m, CD * m + 2 * CD)
             pair = dot3(stack_t, (wh[:, span], wl[:, span]), NN)
             ig[m] = pair[:, :CD]
             ig[m + 1] = pair[:, CD:]
-        for k in range(NX):
-            mates_share(k).start()
+
+    with jax.named_scope("barwait"):
+        pl.semaphore_wait(barrier, NZ - 1 + NY - 1 + NM - 1)
+
+    def offset(j):
+        half = lax.div(j + 1, 2)
+        return half * (2 * lax.rem(j, 2) - 1)
+
+    def to_ring(j):
+        there = lax.rem(z + offset(j) + NZ, NZ)
+        rows = pl.ds(pl.multiple_of(8 * there, 8), 8)
+        return remote(ac.at[me, rows], at.at[me, j], za, j, j, y * NZ + there, me)
+
+    def across_x(k):
+        return remote(ac.at[me], ac.at[me], acx, k, k, dp, across(k))
+
+    def to_mate(k):
+        block = across(-k)
+        return remote(ac.at[block], ac.at[block], acp, k, k, dp, mate)
+
+    def part_across_x(p, k):
+        part = at.at[me, pl.ds(HALF * p, HALF)]
+        return remote(part, part, atx, NX * p + k, NX * p + k, dp, across(k))
+
+    def part_to_mate(p, k):
+        part = at.at[across(-k), pl.ds(HALF * p, HALF)]
+        return remote(part, part, atp, NX * p + k, NX * p + k, dp, mate)
+
+    RIGHT, LEFT = NZ // 2, NZ // 2 - 1
+    TALL = 64 // CHUNKS
+
+    def rightward(s, q):
+        part = ct.at[lax.rem(z - s + 1 + NZ, NZ), pl.ds(TALL * q, TALL)]
+        return remote(part, part, cr, CHUNKS * s + q, CHUNKS * s + q, ring(1), me)
+
+    def leftward(s, q):
+        part = ct.at[lax.rem(z + s - 1, NZ), pl.ds(TALL * q, TALL)]
+        return remote(part, part, cl, CHUNKS * s + q, CHUNKS * s + q, ring(-1), me)
+
+    for q in range(CHUNKS):
+        rightward(1, q).start()
+        leftward(1, q).start()
+
+    def send_channels(first, end):
+        @pl.loop(first, end)
+        def _(j):
+            to_ring(j).start()
+
+    send_channels(1, HALF)
+
+    def mates_share(k):
+        return remote(ig.at[2 * k + 1 - c], rp.at[k], rps, k, k, dp, mate)
+
+    for k in range(NX):
+        mates_share(k).start()
 
     def start_part(p):
         @pl.loop(max(1, HALF * p), HALF * (p + 1))
@@ -323,25 +325,32 @@
     if NZ == 16:
         plan = {
             (1, 1): [(send_channels, HALF, NZ)],
-            (1, last): [(prepare_weights,), (stacks, 0, 1)],
             (2, 0): [(start_part, 0)],
-            (2, last): [(stacks, 1, 3)],
-            (3, last): [(partial_sums,)],
-            (4, 0): [(start_part, 1), (stacks, 3, 5)],
-            (4, last): [(pass_part, 0), (stacks, 5, 7)],
-            (5, last): [(part_here, 0), (leaves, 0, 5), (add_shares,), (start_activations,), (start_shares,)],
-            (6, last): [(pass_part, 1), (leaves, 5, 7), (stacks, 7, 11), (leaves, 7, 8)],
-            (7, last): [(part_here, 1), (leaves, 8, 11), (stacks, 11, 15), (leaves, 11, 15)],
-            (8, last): [(stacks, 15, 16), (leaves, 15, 16)],
+            (2, 3): [(stacks, 1, 3)],
+            (3, 3): [(stacks, 3, 5)],
+            (4, 0): [(start_part, 1)],
+            (4, 2): [(pass_part, 0)],
+            (4, 3): [(stacks, 5, 7)],
+            (5, 1): [(part_here, 0)],
+            (5, 3): [(leaves, 0, 5), (add_shares,), (start_activations,), (start_shares,)],
+            (6, 1): [(pass_part, 1)],
+            (6, 3): [(stacks, 7, 11), (leaves, 5, 8)],
+            (7, 3): [(part_here, 1), (stacks, 11, 15), (leaves, 8, 15)],
+            (8, 3): [(stacks, 15, 16), (leaves, 15, 16)],
         }
     else:
         plan = {
             (RIGHT, last): [
-                (send_channels, HALF, NZ), (prepare_weights,), (partial_sums,),
+                (send_channels, HALF, NZ),
                 (start_part, 0), (add_shares,), (start_part, 1), (start_activations,), (start_shares,),
-                (pass_part, 0), (part_here, 0), (pass_part, 1), (part_here, 1), (stacks, 0, NZ), (leaves, 0, NZ),
+                (pass_part, 0), (part_here, 0), (pass_part, 1), (part_here, 1), (stacks, 1, NZ), (leaves, 0, NZ),
             ],
         }
+
+    merged = {}
+    for (s, q), works in plan.items():
+        merged.setdefault((s, q // 2 if NZ == 16 else q), []).extend(works)
+    plan = merged
 
     for s in range(1, RIGHT + 1):
         for q in range(CHUNKS):
@@ -387,8 +396,6 @@
     on_z = lambda k: (y * NZ + k, me)
     on_y_mp = lambda k: (lax.div(k, NM) * NZ + z, lax.rem(k, NM))
 
-    leave = lambda src, dst, k: pltpu.make_async_copy(src, dst, osem.at[k])
-
     def convolve():
         for k in range(NX):
             to_mate(k).wait_recv()
@@ -401,7 +408,6 @@
             total = moved if total is None else total + moved
         total = jnp.concatenate([total, jnp.zeros_like(total)], axis=0).T
         out_ref[...] = total[:, :64]
-        leave(out_ref, out_hbm, 0).start()
 
     def finish_shares():
         total = ig[me]
@@ -409,7 +415,6 @@
             share(k).wait_recv()
             total = total + rx[lax.rem(x - k + NX, NX)]
         ig_ref[...] = total * gelu_slope(x_ref[...])
-        leave(ig_ref, ig_hbm, 1).start()
 
     with jax.named_scope("gram16"):
         gm[me] = packed(gram(lt, NZ, CG), NZ)
@@ -524,12 +529,8 @@
         fill = -8 * GROUPS % 128
         columns = jnp.concatenate([columns, jnp.zeros((fill, 128), F32)], axis=0).T
         wg_ref[...] = columns[:64, : 8 * GROUPS]
-        leave(wg_ref, wg_hbm, 2).start()
 
     with jax.named_scope("drain"):
-        leave(out_ref, out_hbm, 0).wait()
-        leave(ig_ref, ig_hbm, 1).wait()
-        leave(wg_ref, wg_hbm, 2).wait()
         sent(NY * NM, hm, here, hms, on_y_mp)
         sent(NZ, hz, z, hzs, on_z)
         for j in range(GROUPS):
@@ -558,13 +559,10 @@
             jax.ShapeDtypeStruct((64, 8 * GROUPS), F32),
         ],
         in_specs=[anywhere] * 3,
-        out_specs=[anywhere] * 3,
+        out_specs=[pl.BlockSpec(memory_space=pltpu.VMEM)] * 3,
         scratch_shapes=[
             vmem(PIX, CD),
             vmem(PIX, 64),
-            vmem(PIX, 64),
-            vmem(PIX, CD),
-            vmem(64, 8 * GROUPS),
             vmem(TAPS, 64, NM * CD),
             pltpu.VMEM((STACK, NM * CD), BF16),
             pltpu.VMEM((STACK, NM * CD), BF16),
@@ -587,15 +585,14 @@
             vmem(NY * NM, 1, 128),
             vmem(NZ, 1, 128),
             pltpu.SemaphoreType.DMA((3,)),
-            pltpu.SemaphoreType.DMA((3,)),
             sems(NZ), sems(CHUNKS * NZ), sems(CHUNKS * NZ),
             sems(NX), sems(NX), sems(2 * NX), sems(2 * NX), sems(NX), sems(NX),
             sems(NM), sems(NZ), sems(NY), sems(NY * NM), sems(NZ),
             sems(GROUPS),
         ],
-        compiler_params=pltpu.CompilerParams(collective_id=0, has_side_effects=True),
+        compiler_params=pltpu.CompilerParams(collective_id=0, has_side_effects=True, vmem_limit_bytes=LIMIT),
         name="step",
-    )(preact.reshape(PIX, CD), cotangent.reshape(PIX, 64), weights.transpose(1, 0, 2))
+    )(*(pltpu.with_memory_space_constraint(v, pltpu.HBM) for v in (preact.reshape(PIX, CD), cotangent.reshape(PIX, 64), weights.transpose(1, 0, 2))))
     def hand_over(a, b, d, e, f, g):
         e[...] = a[...]
         f[...] = b[...]
@@ -607,6 +604,7 @@
         out_shape=[jax.ShapeDtypeStruct(v.shape, F32) for v in (output, input_grad, weight_grad)],
         in_specs=[whole] * 3,
         out_specs=[whole] * 3,
+        compiler_params=pltpu.CompilerParams(vmem_limit_bytes=2 * 2**20),
         name="hand_over",
     )(output, input_grad, weight_grad)
     return output.reshape(1, SIDE, SIDE, 64), input_grad.reshape(preact.shape), weight_grad

time: 83.9 us -> 81.3 us (0.969)
  Pallas kernels: 83.1 us -> 80.5 us
    pallas_call x1, Pallas kernels: 81.4 us -> 79.8 us  [local(): pl.pallas_call(functools.partial(kernel, NY, NZ, NX), out_shape=[jax.Shap...]
    pallas_call x1, Pallas kernels: 1.7 us -> 0.74 us  [local(): pl.pallas_call(hand_over, out_shape=[jax.ShapeDtypeStruct(v.shape, F32) f...]
where the time goes in v4:
time: 81.3 us; the launch traced here: 81.2 us
  Pallas kernels  80.5 us (99%)
    pallas_call x1, Pallas kernels, local(): pl.pallas_call(functools.partial(kernel, NY, NZ, NX), out_shape=[jax.Shap...  79.8 us

profile of v4, /device:TPU:1, one launch (start us, length us, event | category | flops | bytes accessed | tf_op | source)
XLA Modules:
  0.0 81.2 jit_solution(10109876301505889598)
XLA Ops:
  0.6 79.8 %step.1 = (f32[256,64]{1,0:T(8,128)S(1)}, f32[256,128]{1,0:T(8,128)S(1)}, f32[64,144]{1,0:T(8,128)S(1)}) custom-call(f32[256,128]{1,0:T(8,128)} %bitcast.6, f32[256,64]{1,0:T(8,128)} %bitcast.7, f32[9,64,1024]{2,1,0:T(8,128)} %bitcast.5), custom_call_target="tpu_custom_call" | custom-call | tf_op jit(solution)/shard_map/step/pallas_call | solution.py:554
  80.4 0.7 hand_over.1

commit v5 on v4

--- a/solution.py
+++ b/solution.py
@@ -328,21 +328,20 @@
             (2, 0): [(start_part, 0)],
             (2, 3): [(stacks, 1, 3)],
             (3, 3): [(stacks, 3, 5)],
-            (4, 0): [(start_part, 1)],
-            (4, 2): [(pass_part, 0)],
+            (4, 0): [(start_part, 1), (start_activations,)],
+            (4, 1): [(pass_part, 0)],
             (4, 3): [(stacks, 5, 7)],
-            (5, 1): [(part_here, 0)],
-            (5, 3): [(leaves, 0, 5), (add_shares,), (start_activations,), (start_shares,)],
+            (5, 3): [(part_here, 0), (leaves, 0, 5), (add_shares,)],
             (6, 1): [(pass_part, 1)],
             (6, 3): [(stacks, 7, 11), (leaves, 5, 8)],
-            (7, 3): [(part_here, 1), (stacks, 11, 15), (leaves, 8, 15)],
+            (7, 3): [(stacks, 11, 15), (part_here, 1), (leaves, 8, 15)],
             (8, 3): [(stacks, 15, 16), (leaves, 15, 16)],
         }
     else:
         plan = {
             (RIGHT, last): [
                 (send_channels, HALF, NZ),
-                (start_part, 0), (add_shares,), (start_part, 1), (start_activations,), (start_shares,),
+                (start_part, 0), (add_shares,), (start_part, 1), (start_activations,),
                 (pass_part, 0), (part_here, 0), (pass_part, 1), (part_here, 1), (stacks, 1, NZ), (leaves, 0, NZ),
             ],
         }
@@ -396,6 +395,10 @@
     on_z = lambda k: (y * NZ + k, me)
     on_y_mp = lambda k: (lax.div(k, NM) * NZ + z, lax.rem(k, NM))
 
+    def share_and_convolve():
+        start_shares()
+        convolve()
+
     def convolve():
         for k in range(NX):
             to_mate(k).wait_recv()
@@ -421,7 +424,7 @@
     with jax.named_scope("g16mp"):
         gz[z] = exchange(gm, NM, me, gms, on_mp, pass_activations)
     with jax.named_scope("g16z"):
-        table = exchange(gz, NZ, z, gzs, on_z, convolve)
+        table = exchange(gz, NZ, z, gzs, on_z, share_and_convolve)
     with jax.named_scope("coef16"):
         table = unpacked(table, NZ, cb)
         rows = table.shape[0]

time: 81.3 us -> 81.3 us (level)
  no operation moved by 1% of the time
where the time goes in v5:
time: 81.3 us; the launch traced here: 81.1 us
  Pallas kernels  80.5 us (99%)
    pallas_call x1, Pallas kernels, local(): pl.pallas_call(functools.partial(kernel, NY, NZ, NX), out_shape=[jax.Shap...  79.8 us

profile of v5, /device:TPU:1, one launch (start us, length us, event | category | flops | bytes accessed | tf_op | source)
XLA Modules:
  0.0 81.1 jit_solution(74815459576736466)
XLA Ops:
  0.6 79.8 %step.1 = (f32[256,64]{1,0:T(8,128)S(1)}, f32[256,128]{1,0:T(8,128)S(1)}, f32[64,144]{1,0:T(8,128)S(1)}) custom-call(f32[256,128]{1,0:T(8,128)} %bitcast.6, f32[256,64]{1,0:T(8,128)} %bitcast.7, f32[9,64,1024]{2,1,0:T(8,128)} %bitcast.5), custom_call_target="tpu_custom_call" | custom-call | tf_op jit(solution)/shard_map/step/pallas_call | solution.py:557
  80.4 0.7 hand_over.1
